TPU v7x, 512 devices: a whole 4x4x16 slice. The times are simulated.
512 devices in a mesh: branch: 4 (over y_hi, core), segment: 8 (over y_lo, x), tp: 16 (over z).
Axes of the slice: x: 4, y: 4 (y_hi: 2, y_lo: 2; y = y_hi * 2 + y_lo), z: 16, core: 2. Of those that a mesh axis runs over, the one named last changes fastest.
Arguments:
- rollout: bfloat16 [2304, 8192], P(('branch', 'segment')), may hold values from -6 to 6
- send_rows: int32 [2304], P(('branch', 'segment')), may hold values from 0 to 71, as said below
- seq_lengths: int32 [8, 6], P('segment'), may hold values from 1 to 144, 288 in all within a row
- attn_gain: bfloat16 [4, 8192], P('branch'), may hold values from 0.099609375 to 1.8984375
- w_query: bfloat16 [4, 8192, 8192], P('branch', 'segment', 'tp'), may hold values from -1 to 1
- w_keyval: bfloat16 [4, 8192, 2048], P('branch', 'segment', 'tp'), may hold values from -1 to 1
- head_weight: bfloat16 [4, 8192], P('branch', 'tp'), may hold values from -0.0625 to 0.0625
- head_attn: bfloat16 [4, 8192], P('branch', 'tp'), may hold values from -0.25 to 0.25
Outputs:
- scores: float32 [4, 2304], P(None, ('branch', 'segment'))
Inputs may be any that keep to these rules, and one draw needn't show every extreme that they name: `send_rows`: each aligned block of 72 entries holds every number of 0 to 71 once.
All inputs are finite; a program needn't handle non-finite values.
Results may differ from a plain program's by a relative error of at most 0.006.
Values may be sent and summed in bfloat16 or wider, within the bound.
A program may use at most 128 MiB of HBM per device.

v0:
```python
import math

import jax
import jax.numpy as jnp
from jax import lax
from jax.sharding import PartitionSpec as P

HEAD = 128
HEADS = 64
KV_HEADS = 8


epsilon = 1e-05


def local(rollout, send_rows, seq_lengths, attn_gain, w_query, w_keyval, head_weight, head_attn):
    n_branch = lax.axis_size("branch")
    n_segment = lax.axis_size("segment")
    gen_rows = rollout.shape[0]
    piece_rows = gen_rows // n_segment
    row_width = rollout.shape[1]
    ordered = jnp.take(rollout, send_rows, axis=0).reshape(n_segment, piece_rows, row_width)
    copies = jnp.broadcast_to(ordered[None], (n_branch, n_segment, piece_rows, row_width))
    copies = copies.reshape(n_branch * n_segment, piece_rows, row_width)
    arrived = lax.all_to_all(copies, ("branch", "segment"), split_axis=0, concat_axis=0, tiled=True)
    packed = arrived.reshape(-1, row_width)
    pack_rows = packed.shape[0]
    rows_float = packed.astype(jnp.float32)
    mean_square = jnp.mean(rows_float * rows_float, axis=-1, keepdims=True)
    normed = (
        rows_float * lax.rsqrt(mean_square + epsilon) * attn_gain[0].astype(jnp.float32)
    ).astype(jnp.bfloat16)
    query_acc = jnp.dot(
        normed,
        lax.all_gather(w_query, "segment", axis=1, tiled=True)[0],
        preferred_element_type=jnp.float32,
    )
    keyval_acc = jnp.dot(
        normed,
        lax.all_gather(w_keyval, "segment", axis=1, tiled=True)[0],
        preferred_element_type=jnp.float32,
    )
    queries = query_acc.astype(jnp.bfloat16)
    keyval_part = keyval_acc.astype(jnp.bfloat16)
    keyval = lax.all_gather(keyval_part, "tp", axis=1, tiled=True)
    tp_index = lax.axis_index("tp")
    heads_here = queries.shape[1] // HEAD
    group_size = HEADS // KV_HEADS
    per_group = min(heads_here, group_size)
    group_span = heads_here // per_group
    kv_first = tp_index * heads_here // group_size
    key_rows = lax.dynamic_slice_in_dim(keyval, kv_first * HEAD, group_span * HEAD, 1)
    value_rows = lax.dynamic_slice_in_dim(
        keyval, KV_HEADS * HEAD + kv_first * HEAD, group_span * HEAD, 1
    )
    key_rows = key_rows.reshape(pack_rows, group_span, HEAD)
    value_rows = value_rows.reshape(pack_rows, group_span, HEAD)
    queries = queries.reshape(pack_rows, group_span, per_group, HEAD)
    positions = jnp.arange(pack_rows, dtype=jnp.int32)
    doc_ends = jnp.cumsum(seq_lengths[0])
    doc_ids = jnp.sum((positions[:, None] >= doc_ends[None, :]).astype(jnp.int32), axis=-1)
    visible = (doc_ids[:, None] == doc_ids[None, :]) & (positions[None, :] <= positions[:, None])
    logits = jnp.einsum(
        "qgpc,kgc->gpqk", queries, key_rows, preferred_element_type=jnp.float32
    ) / math.sqrt(HEAD)
    logits = jnp.where(visible[None, None], logits, -1e30)
    row_max = jnp.max(logits, axis=-1, keepdims=True)
    expo = jnp.exp(logits - row_max)
    probabilities = (expo / jnp.sum(expo, axis=-1, keepdims=True)).astype(jnp.bfloat16)
    attended = jnp.einsum(
        "gpqk,kgc->qgpc", probabilities, value_rows, preferred_element_type=jnp.float32
    )
    attended = attended.reshape(pack_rows, heads_here * HEAD)
    slice_width = head_weight.shape[1]
    own_columns = lax.dynamic_slice_in_dim(packed, tp_index * slice_width, slice_width, 1)
    direct = jnp.dot(own_columns, head_weight[0], preferred_element_type=jnp.float32)
    through = jnp.dot(attended, head_attn[0].astype(jnp.float32), precision=lax.Precision.HIGHEST)
    totals = lax.psum(direct + through, "tp")
    outgoing = totals.reshape(n_branch * n_segment, piece_rows)
    incoming = lax.all_to_all(
        outgoing, ("branch", "segment"), split_axis=0, concat_axis=0, tiled=True
    )
    incoming = incoming.reshape(n_branch, n_segment * piece_rows)
    scores = jnp.zeros((n_branch, gen_rows), jnp.float32).at[:, send_rows].set(incoming)
    return scores


def solution(mesh):
    return jax.shard_map(
        local,
        mesh=mesh,
        in_specs=(
            P(("branch", "segment"), None),
            P(("branch", "segment")),
            P("segment", None),
            P("branch", None),
            P("branch", "segment", "tp"),
            P("branch", "segment", "tp"),
            P("branch", "tp"),
            P("branch", "tp"),
        ),
        out_specs=P(None, ("branch", "segment")),
        check_vma=False,
    )
```

profile of v0, /device:TPU:1, one launch (start us, length us, event | category | flops | bytes accessed | tf_op | source)
XLA Modules:
  0.0 387.5 jit_solution(12303742169167186144)
XLA Ops:
  6.5 0.0 copy-start
  6.5 0.0 all-gather.4.cloned.1.call-start
  6.5 0.7 all-gather.4.cloned.1.call-update
  7.3 0.0 all-gather.8.cloned.1.call-start
  7.3 0.7 all-gather.8.cloned.1.call-update
  8.0 0.7 compare_select_fusion
  8.7 0.0 copy-done
  8.7 2.4 gather_fusion
  11.1 0.0 copy-start.4
  11.1 1.8 gather.7
  12.9 0.0 copy-done.4
  12.9 0.1 broadcast_in_dim.48
  13.0 0.3 broadcast_select_fusion
  13.3 4.4 %broadcast_in_dim.51 = bf16[4,8,9,8192]{3,2,1,0:T(8,128)(2,1)} broadcast(bf16[8,9,8192]{2,1,0:T(8,128)(2,1)S(1)} %broadcast_select_fusion), dimensions={1,2,3} | broadcast | bytes 5898240 | tf_op jit(solution)/shard_map/broadcast_in_dim | solution.py:23
  17.7 0.0 copy-start.1
  17.7 11.6 %all-to-all-start = ((bf16[32,9,8192]{2,1,0:T(8,128)(2,1)}), bf16[32,9,8192]{2,1,0:T(8,128)(2,1)}, u32[]{:S(2)}, u32[]{:S(2)}) async-start(bf16[32,9,8192]{2,1,0:T(8,128)(2,1)} %bitcast.58), calls=%async_computation | async-start | bytes 16777216 | tf_op jit(solution)/shard_map/all_to_all | solution.py:25
  29.4 0.2 all-gather.6.cloned.1.call-start
  29.6 0.0 copy-done.1
  29.6 144.8 %all-to-all-done = bf16[32,9,8192]{2,1,0:T(8,128)(2,1)} async-done(((bf16[32,9,8192]{2,1,0:T(8,128)(2,1)}), bf16[32,9,8192]{2,1,0:T(8,128)(2,1)}, u32[]{:S(2)}, u32[]{:S(2)}) %all-to-all-start) | async-done | bytes 4718624 | tf_op jit(solution)/shard_map/all_to_all | solution.py:25
  174.5 5.4 %fusion = f32[32,9]{1,0:T(8,128)S(1)} fusion(bf16[32,9,8192]{2,1,0:T(8,128)(2,1)} %all-to-all-done), kind=kLoop, calls=%fused_computation.4 | loop fusion | flops 7077600 | bytes 4719744 | tf_op jit(solution)/shard_map/reduce_sum | solution.py:29
  179.9 9.9 %fusion.2 = bf16[32,9,8192]{2,1,0:T(8,128)(2,1)} fusion(bf16[32,9,8192]{2,1,0:T(8,128)(2,1)} %all-to-all-done, f32[8192]{0:T(1024)S(1)} %bitcast.60, f32[32,9]{1,0:T(8,128)S(1)} %add_rsqrt_fusion), kind=kLoop, calls=%fused_computation.6 | loop fusion | flops 9437184 | bytes 9471104 | tf_op jit(solution)/shard_map/convert_element_type | solution.py:32
  189.9 6.9 %convert_element_type.30 = bf16[288,8192]{1,0:T(8,128)(2,1)} reshape(bf16[32,9,8192]{2,1,0:T(8,128)(2,1)} %fusion.2) | data formatting | bytes 9437184 | tf_op jit(solution)/shard_map/convert_element_type | solution.py:32
  196.8 0.0 copy-start.5
  196.8 0.0 all-gather.4.cloned.1.call-done
  196.8 5.1 %fusion.14 = bf16[288,128]{1,0:T(8,128)(2,1)} fusion(bf16[288,8192]{1,0:T(8,128)(2,1)} %convert_element_type.30, bf16[1,8192,128]{2,1,0:T(8,128)(2,1)} %all-gather.4.cloned.1.call-done), kind=kOutput, calls=%fused_computation.19 | convolution fusion | flops 604016640 | bytes 6889472 | tf_op jit(solution)/shard_map/dot_general | solution.py:38
  202.0 0.0 all-gather.6.cloned.1.call-update
  202.0 0.0 copy-done.5
  202.0 0.2 reduce-window.8
  202.2 0.1 convert_reduce_fusion
  202.3 0.1 fusion.20
  202.4 0.0 copy-start.2
  202.4 6.9 %reshape.163 = bf16[288,8192]{1,0:T(8,128)(2,1)} reshape(bf16[32,9,8192]{2,1,0:T(8,128)(2,1)} %all-to-all-done) | data formatting | bytes 9437184 | tf_op jit(solution)/shard_map/reshape | solution.py:26
  209.3 0.0 copy-done.2
  209.3 1.2 convolution_reduce_fusion.1
  210.5 17.9 %all-gather.8.cloned.1.call-done = bf16[1,8192,512]{2,1,0:T(8,128)(2,1)} async-done(((bf16[1,1024,512]{2,1,0:T(8,128)(2,1)}), bf16[1,8192,512]{2,1,0:T(8,128)(2,1)}) %all-gather.8.cloned.1.call-update) | async-done | bytes 8388624 | tf_op jit(solution)/shard_map/all_gather | solution.py:35
  228.4 7.4 %fusion.11 = bf16[36,4,8,128]{3,2,1,0:T(8,128)(2,1)S(1)} fusion(bf16[288,8192]{1,0:T(8,128)(2,1)} %convert_element_type.30, bf16[1,8192,512]{2,1,0:T(8,128)(2,1)} %all-gather.8.cloned.1.call-done), kind=kOutput, calls=%fused_computation.18 | convolution fusion | flops 2416066560 | bytes 13402112 | tf_op jit(solution)/shard_map/dot_general | solution.py:33
  235.8 58.6 %all-gather.6.cloned.1.call-done = bf16[288,2048]{1,0:T(8,128)(2,1)} async-done(((bf16[288,128]{1,0:T(8,128)(2,1)}), bf16[288,2048]{1,0:T(8,128)(2,1)}) %all-gather.6.cloned.1.call-update) | async-done | bytes 1179664 | tf_op jit(solution)/shard_map/all_gather | solution.py:45
  294.4 1.4 fusion.35
  295.8 0.3 fusion.7
  296.1 0.0 copy-start.3
  296.1 1.5 convolution_bitcast_fusion
  297.5 0.4 copy.25
  297.9 0.0 copy-done.3
  297.9 0.4 convolution_reduce_fusion
  298.4 0.1 all_to_all.10
  298.5 40.6 %psum.7 = f32[32,1,9]{2,0,1:T(8,128)S(1)} all-reduce(f32[32,1,9]{2,0,1:T(8,128)S(1)} %all_to_all.10), channel_id=1, replica_groups=mesh['branch'=4,'segment'=8,'tp'=16] {'tp'}, use_global_device_ids=true, to_apply=%region_5.6 | all-reduce | flops 288 | bytes 2304 | tf_op jit(solution)/shard_map/psum | solution.py:78
  339.0 39.1 %all_to_all.14 = f32[32,1,9]{2,1,0:T(1,128)S(1)} all-to-all(f32[32,1,9]{2,1,0:T(1,128)S(1)} %bitcast.61), channel_id=1, replica_groups=mesh['branch'=4,'segment'=8,'tp'=16] {'branch','segment'}, dimensions={0} | all-to-all | bytes 2304 | tf_op jit(solution)/shard_map/all_to_all | solution.py:80
  378.2 0.5 broadcast.79
  378.7 0.7 reduce.10
  379.4 0.1 reshape.180
  379.4 0.1 copy.27
  379.6 0.7 scatter_custom_fusion
  380.3 0.7 copy.28
  (5 shorter events, 0.1 us)
Async XLA Ops:
  6.5 2.1 copy-start
  6.5 190.3 %all-gather.4.cloned.1.call-start = ((), (), s32[]{:S(2)}) async-start(), calls=%async_computation.2 | async-start | bytes 2359296 | tf_op jit(solution)/shard_map/all_gather | solution.py:40
  7.3 221.2 %all-gather.8.cloned.1.call-start = ((), (), s32[]{:S(2)}) async-start(), calls=%async_computation.4 | async-start | bytes 9437184 | tf_op jit(solution)/shard_map/all_gather | solution.py:35
  11.1 1.8 copy-start.4
  17.7 11.9 %copy-start.1 = (bf16[1,8192]{1,0:T(2,128)(2,1)S(1)}, bf16[1,8192]{1,0:T(2,128)(2,1)}, u32[]{:S(2)}) copy-start(bf16[1,8192]{1,0:T(2,128)(2,1)} %param.11) | copy-start | bytes 49156
  17.7 156.7 %all-to-all-start = ((bf16[32,9,8192]{2,1,0:T(8,128)(2,1)}), bf16[32,9,8192]{2,1,0:T(8,128)(2,1)}, u32[]{:S(2)}, u32[]{:S(2)}) async-start(bf16[32,9,8192]{2,1,0:T(8,128)(2,1)} %bitcast.58), calls=%async_computation | async-start | bytes 16777216 | tf_op jit(solution)/shard_map/all_to_all | solution.py:25
  29.4 265.0 %all-gather.6.cloned.1.call-start = ((), (), s32[]{:S(2)}) async-start(), calls=%async_computation.3 | async-start | bytes 1253376 | tf_op jit(solution)/shard_map/all_gather | solution.py:45
  196.8 5.2 %copy-start.5 = (s32[1,6]{1,0:T(1,128)S(1)}, s32[1,6]{1,0:T(1,128)}, u32[]{:S(2)}) copy-start(s32[1,6]{1,0:T(1,128)} %param.10) | copy-start | bytes 76
  202.4 6.9 %copy-start.2 = (bf16[1,512]{1,0:T(2,128)(2,1)S(1)}, bf16[1,512]{1,0:T(2,128)(2,1)}, u32[]{:S(2)}) copy-start(bf16[1,512]{1,0:T(2,128)(2,1)} %param.14) | copy-start | bytes 3076
  296.1 1.9 copy-start.3
Sparse Core Ops, SparseCore 0:
  9.4 92.1 all-gather.3
  103.7 124.6 all-gather.7
  230.4 63.9 all-gather.5
where the time goes:
time: 388 us; the launch traced here: 387 us
  waiting for transfers between devices  223 us (57%)
  blocking collectives  79.7 us (21%)
  local copies, waits for them, and re-layouts  25.2 us (6%)
  other arithmetic  17.7 us (5%)
  matrix products  17 us (4%)
  between operations  13.3 us (3%)
  starting transfers between devices  11.9 us (3%)
    all_to_all x1, waiting for transfers between devices, local(): lax.all_to_all(copies, ('branch', 'segment'), split_axis=0, concat_axis=0...  145 us
    all_gather x1, waiting for transfers between devices, local(): keyval = lax.all_gather(keyval_part, 'tp', axis=1, tiled=True)  58.6 us
    psum x1, blocking collectives, local(): totals = lax.psum(direct + through, 'tp')  40.6 us
    all_to_all x1, blocking collectives, local(): lax.all_to_all(outgoing, ('branch', 'segment'), split_axis=0, concat_axis...  39.1 us
    all_gather x1, waiting for transfers between devices, local(): lax.all_gather(w_query, 'segment', axis=1, tiled=True)[0]  17.9 us
    all_to_all x1, starting transfers between devices, local(): lax.all_to_all(copies, ('branch', 'segment'), split_axis=0, concat_axis=0...  11.6 us
    convert_element_type x1, other arithmetic, local(): normed = (rows_float * lax.rsqrt(mean_square + epsilon) * attn_gain[0].as...  9.94 us
  transfers between devices with their start and end apart: 4, of which 3 were waited for; matrix products, arithmetic and copies ran while one was open for 14% of the time, Pallas kernels for 0%

commit v1 on v0

v1 whole, which is shorter than its diff:
```python
import math

import jax
import jax.numpy as jnp
from jax import lax
from jax.experimental import pallas as pl
from jax.experimental.pallas import tpu as pltpu
from jax.sharding import PartitionSpec as P

HEAD = 128
EPS = 1e-05
MESH = pl.DeviceIdType.MESH

BR, SEG, TP = 4, 8, 16
ROWS = 72
PIECE = 9
PACK = 288
D = 8192
KS = D // SEG
HK = KS // 2
QC = 512
KC = 128
CC = QC + KC
MSG = 80
LANES = 128


def kernel(order_ref, orow_ref, len_ref, roll_hbm, gain_hbm, wq_hbm, wkv_hbm, hw_hbm, ha_hbm, out_ref,
           roll, gain_v, wq, wkv, hw_v, ha_v,
           y, X, pf, pbuf, rbuf, lbuf, fbuf, qbuf, kvown, kvb, hwf, hwb, bias, tb, rb, zo, zb,
           ld, xr, ds, fs, rs, sf, ps, pr, hs, hr, kvs, kvr, ts, tr, zs, zr):
    br = lax.axis_index("branch")
    seg = lax.axis_index("segment")
    z = lax.axis_index("tp")
    core = lax.rem(br, 2)
    sib = br + 1 - 2 * core
    step_z = 1 - 2 * core
    nxt = lax.rem(z + step_z + TP, TP)
    a0 = z // 2
    half = lax.rem(z, 2)
    source = seg == a0
    f32, bf = jnp.float32, jnp.bfloat16

    ld_roll = pltpu.make_async_copy(roll_hbm, roll, ld.at[0])
    ld_wq = pltpu.make_async_copy(wq_hbm, wq, ld.at[1])
    ld_wkv = pltpu.make_async_copy(wkv_hbm, wkv, ld.at[2])
    ld_gain = pltpu.make_async_copy(gain_hbm, gain_v, ld.at[3])
    ld_hw = pltpu.make_async_copy(hw_hbm, hw_v, ld.at[4])
    ld_ha = pltpu.make_async_copy(ha_hbm, ha_v, ld.at[5])
    for c in (ld_roll, ld_hw, ld_gain, ld_wq, ld_wkv, ld_ha):
        c.start()

    barrier = pltpu.get_barrier_semaphore()

    def greet(dev):
        pl.semaphore_signal(barrier, inc=1, device_id=dev, device_id_type=MESH)

    for o in range(BR):
        for d in range(SEG):
            if o or d:
                greet((lax.rem(br + o, BR), lax.rem(seg + d, SEG), z))
    for d in range(1, TP):
        greet((br, seg, lax.rem(z + d, TP)))

    ld_roll.wait()

    @pl.when(source)
    def _():
        xf = roll[...].astype(f32)
        ms = jnp.sum(xf * xf, axis=-1, keepdims=True) * (1.0 / D)
        r = lax.rsqrt(ms + EPS)
        sub = lax.broadcasted_iota(jnp.int32, (ROWS, LANES), 0)
        r_row = jnp.sum(jnp.where(orow_ref[...] == sub, r, 0.0), axis=0, keepdims=True)
        hi = r_row.astype(bf).astype(f32)
        mid = (r_row - hi).astype(bf).astype(f32)
        lo = r_row - hi - mid
        s8 = lax.broadcasted_iota(jnp.int32, (8, LANES), 0)
        tail = jnp.where(s8 == 0, hi, jnp.where(s8 == 1, mid, jnp.where(s8 == 2, lo, 0.0)))
        tail = jnp.concatenate([tail] + [jnp.zeros((8, LANES), f32)] * (HK // LANES - 1), axis=1)
        lane = lax.broadcasted_iota(jnp.int32, (ROWS, ROWS), 1)
        perm = (order_ref[...] == lane).astype(f32).astype(bf)
        for c in range(2 * SEG):
            yc = jnp.dot(perm, roll[:, c * HK:(c + 1) * HK], preferred_element_type=f32)
            y[c] = jnp.concatenate([yc, tail], axis=0).astype(bf)

    ld_hw.wait()
    hwf[...] = hw_v[...].astype(f32)

    pl.semaphore_wait(barrier, BR * SEG - 1 + TP - 1)

    def dist(d, o):
        s = lax.rem(seg + d, SEG)
        return pltpu.make_async_remote_copy(
            src_ref=y.at[2 * s + half], dst_ref=X.at[z, br], send_sem=ds.at[2 * d + o], recv_sem=xr.at[z, br],
            device_id=(lax.rem(br + 2 * o, 4), s, z), device_id_type=MESH)

    own = pltpu.make_async_copy(y.at[2 * seg + half], X.at[z, br], xr.at[z, br])

    @pl.when(source)
    def _():
        own.start()
        for d in range(SEG):
            for o in range(2):
                if d or o:
                    dist(d, o).start()

    def hw_send(o):
        return pltpu.make_async_remote_copy(
            src_ref=hwf, dst_ref=hwb.at[br], send_sem=hs.at[o - 1], recv_sem=hr.at[br],
            device_id=(lax.rem(br + o, BR), seg, z), device_id_type=MESH)

    for o in range(1, BR):
        hw_send(o).start()

    def piece(b):
        return pltpu.make_async_copy(X.at[z, b], X.at[z, b], xr.at[z, b])

    def to_sib(b, k):
        return pltpu.make_async_remote_copy(
            src_ref=X.at[z, b], dst_ref=X.at[z, b], send_sem=fs.at[k], recv_sem=xr.at[z, b],
            device_id=(sib, seg, z), device_id_type=MESH)

    for c in (ld_gain, ld_wq, ld_wkv, ld_ha):
        c.wait()

    rq = lax.broadcasted_iota(jnp.int32, (PACK, PACK), 0)
    rk = lax.broadcasted_iota(jnp.int32, (PACK, PACK), 1)

    def position(r):
        main = (((r >> 3) & 3) * SEG + (r >> 5)) * PIECE + (r & 7)
        left = ((r & 3) * SEG + ((r - 256) >> 2)) * PIECE + 8
        return jnp.where(r < 256, main, left)

    pq, pk = position(rq), position(rk)
    start = jnp.zeros((PACK, PACK), jnp.int32)
    end = jnp.int32(0)
    for e in range(len_ref.shape[1]):
        end = end + len_ref[0, e]
        start = jnp.where(pq >= end, end, start)
    bias[...] = jnp.where((pk >= start) & (pk <= pq), 0.0, -1e30)

    for k in range(2):
        b = core + 2 * k
        piece(b).wait()
        to_sib(b, k).start()
    for k in range(2):
        piece(1 - core + 2 * k).wait()

    def ring(blk, t, h):
        return pltpu.make_async_remote_copy(
            src_ref=X.at[blk, pl.ds(2 * h, 2)], dst_ref=X.at[blk, pl.ds(2 * h, 2)], send_sem=rs.at[t, h],
            recv_sem=xr.at[blk, 2 * h], device_id=(br, seg, nxt), device_id_type=MESH)

    def side(blk, t, h):
        return pltpu.make_async_remote_copy(
            src_ref=X.at[blk, pl.ds(2 * h, 2)], dst_ref=X.at[blk, pl.ds(2 * h, 2)], send_sem=sf.at[t, h],
            recv_sem=xr.at[blk, 2 * h], device_id=(sib, seg, z), device_id_type=MESH)

    for h in range(2):
        ring(z, 0, h).start()

    def psend(t, d, a):
        s = lax.rem(seg + d, SEG)
        return pltpu.make_async_remote_copy(
            src_ref=pbuf.at[t, d - 1], dst_ref=rbuf.at[d - 1, a], send_sem=ps.at[t, d - 1], recv_sem=pr.at[d - 1, a],
            device_id=(br, s, z), device_id_type=MESH)

    odd = 2 * half - 1
    dj = lax.broadcasted_iota(jnp.int32, (ROWS, LANES), 0) == lax.broadcasted_iota(jnp.int32, (ROWS, LANES), 1)

    def step(t, _):
        mine = lax.rem(z - step_z * t + TP, TP)
        their = lax.rem(z + step_z * t + TP, TP)
        has = jnp.logical_or(t < 8, core == 0)
        fwd = jnp.logical_or(t < 7, jnp.logical_and(t < 8, core == 0))
        has_side = jnp.logical_or(t < 8, core == 1)
        for h in range(2):
            @pl.when(has)
            def _():
                ring(mine, t, h).wait_recv()

            @pl.when(fwd)
            def _():
                ring(mine, t, h).start()

            @pl.when(has)
            def _():
                side(mine, t, h).start()

        @pl.when(has_side)
        def _():
            for h in range(2):
                side(their, t, h).wait_recv()

        off = t // 2
        sign = jnp.where(lax.rem(t, 2) == 0, odd, -odd)
        a = lax.rem(a0 + sign * off + SEG, SEG)
        scale = []
        for r in range(BR):
            row = jnp.sum(X[2 * a, r][ROWS:, :LANES].astype(f32), axis=0, keepdims=True)
            scale.append(jnp.sum(jnp.where(dj, row, 0.0), axis=-1, keepdims=True))
        acc = None
        for b in range(2):
            g0 = pl.multiple_of(seg * KS + b * HK, HK)
            gain = gain_v[:, pl.ds(g0, HK)].astype(f32)
            xf = jnp.concatenate([X[2 * a + b, r].astype(f32)[:ROWS] * scale[r] for r in range(BR)], axis=0)
            lhs = (xf * gain).astype(bf)
            dq = jnp.dot(lhs, wq[b * HK:(b + 1) * HK, :], preferred_element_type=f32)
            dk = jnp.dot(lhs, wkv[b * HK:(b + 1) * HK, :], preferred_element_type=f32)
            acc = (dq, dk) if acc is None else (acc[0] + dq, acc[1] + dk)
        pf[:, :, :, :QC] = acc[0].reshape(BR, PIECE, 8, QC)
        pf[:, :, :, QC:] = acc[1].reshape(BR, PIECE, 8, KC)
        for d in range(1, SEG):
            s = lax.rem(seg + d, SEG)
            pbuf[t - 1, d - 1] = pf[:, s].reshape(32, CC).astype(bf)
            psend(t - 1, d, a).start()
        fbuf[a] = pf[:, seg].reshape(32, CC)
        for c in range(CC // LANES):
            lbuf[c, pl.ds(pl.multiple_of(a * 32, 32), 32), :] = pf[:, 8, :, c * LANES:(c + 1) * LANES].reshape(32, LANES)
        return 0

    lax.fori_loop(1, 9, step, 0)

    for s in range(SEG):
        v = jnp.concatenate([lbuf[c, pl.ds(s, 32, stride=8), :] for c in range(CC // LANES)], axis=1)
        at = lax.rem(s - seg + SEG, SEG)

        @pl.when(at == 0)
        def _():
            fbuf[8] = v

        @pl.when(at > 0)
        def _():
            pbuf[8, at - 1] = v.astype(bf)
    for d in range(1, SEG):
        psend(8, d, 8).start()

    for o in range(1, BR):
        frm = lax.rem(br + o, BR)
        pltpu.make_async_copy(hwb.at[frm], hwb.at[frm], hr.at[frm]).wait()
    hwb[br] = hwf[...]
    hw4 = jnp.concatenate([hwb[m] for m in range(BR)] + [jnp.zeros((4, QC), f32)], axis=0).astype(bf)
    c0 = pl.multiple_of(z * QC, QC)
    direct = lax.dot_general(hw4, roll[:, pl.ds(c0, QC)], (((1,), (1,)), ((), ())), preferred_element_type=f32)
    lanes16 = lax.broadcasted_iota(jnp.int32, (16, LANES), 1)
    left_ord = order_ref[64:72, :]
    table = jnp.concatenate(
        [jnp.concatenate([order_ref[s * 8:(s + 1) * 8, :], left_ord], axis=0) == lanes16 for s in range(SEG)], axis=1)
    table = table.astype(f32).astype(bf)

    def kv_sum(c, _):
        tot = fbuf[c, :, QC:]
        for d in range(1, SEG):
            psend(8, d, c).wait_recv()
            tot = tot + rbuf[d - 1, c, :, QC:].astype(f32)
        kvown[pl.ds(pl.multiple_of(c * 32, 32), 32), :] = tot.astype(bf)
        return 0

    lax.fori_loop(0, 9, kv_sum, 0)
    slot = z // 8

    def kv_send(e):
        return pltpu.make_async_remote_copy(
            src_ref=kvown, dst_ref=kvb.at[slot], send_sem=kvs.at[e], recv_sem=kvr.at[slot],
            device_id=(br, seg, 2 * lax.rem(z, 8) + e), device_id_type=MESH)

    keep = pltpu.make_async_copy(kvown, kvb.at[slot], kvr.at[slot])
    for e in range(2):
        here = 2 * lax.rem(z, 8) + e == z

        @pl.when(here)
        def _():
            keep.start()

        @pl.when(jnp.logical_not(here))
        def _():
            kv_send(e).start()

    def q_sum(c, _):
        tot = fbuf[c, :, :QC]
        for d in range(1, SEG):
            tot = tot + rbuf[d - 1, c, :, :QC].astype(f32)
        qbuf[pl.ds(pl.multiple_of(c * 32, 32), 32), :] = tot.astype(bf)
        return 0

    lax.fori_loop(0, 9, q_sum, 0)

    for k in range(2):
        pltpu.make_async_copy(kvb.at[k], kvb.at[k], kvr.at[k]).wait()
    keys, values = kvb[0], kvb[1]
    acc = jnp.zeros((PACK, HEAD), f32)
    for h in range(QC // HEAD):
        logits = lax.dot_general(qbuf[:, h * HEAD:(h + 1) * HEAD], keys, (((1,), (1,)), ((), ())),
                                 preferred_element_type=f32)
        logits = logits * (1.0 / math.sqrt(HEAD)) + bias[...]
        expo = jnp.exp(logits - jnp.max(logits, axis=-1, keepdims=True))
        probs = (expo * (1.0 / jnp.sum(expo, axis=-1, keepdims=True))).astype(bf)
        att = jnp.dot(probs, values, preferred_element_type=f32)
        acc = acc + att * ha_v[:, h * HEAD:(h + 1) * HEAD].astype(f32)
    through = jnp.sum(acc, axis=-1, keepdims=True)
    sub = lax.broadcasted_iota(jnp.int32, (256, LANES), 0)
    lane = lax.broadcasted_iota(jnp.int32, (256, LANES), 1)
    main = jnp.where((sub & 7) == lane, through[:256], 0.0).reshape(32, 8, LANES).sum(axis=1)
    main = main + jnp.where(lane[:32] == 8 + seg, through[256:], 0.0)
    tb[...] = main.reshape(32, 1, LANES)

    def tsend(o, d):
        b2, s2 = lax.rem(br + o, BR), lax.rem(seg + d, SEG)
        return pltpu.make_async_remote_copy(
            src_ref=tb.at[s2 * BR + b2], dst_ref=rb.at[br * SEG + seg], send_sem=ts, recv_sem=tr,
            device_id=(b2, s2, z), device_id_type=MESH)

    for o in range(BR):
        for d in range(SEG):
            if o or d:
                tsend(o, d).start()
    pltpu.make_async_copy(tb.at[seg * BR + br], rb.at[br * SEG + seg], tr).start()
    pltpu.make_async_copy(rb, rb, tr).wait()
    got = rb[...].reshape(32, LANES)[:, :16]
    g_hi = got.astype(bf)
    rest = got - g_hi.astype(f32)
    g_mid = rest.astype(bf)
    g_lo = (rest - g_mid.astype(f32)).astype(bf)
    routed = jnp.dot(g_hi, table, preferred_element_type=f32)
    routed = routed + jnp.dot(g_mid, table, preferred_element_type=f32)
    routed = routed + jnp.dot(g_lo, table, preferred_element_type=f32)
    pack_of = lax.broadcasted_iota(jnp.int32, (32, LANES), 0) & 7
    part = jnp.zeros((32, LANES), f32)
    for s in range(SEG):
        part = part + jnp.where(pack_of == s, routed[:, s * LANES:(s + 1) * LANES], 0.0)
    part = part.reshape(BR, SEG, LANES).sum(axis=1)
    zo[...] = jnp.zeros((8, LANES), f32)
    zo[:BR, :ROWS] = part[:, :ROWS] + direct[:BR]

    def zsend(d):
        return pltpu.make_async_remote_copy(
            src_ref=zo, dst_ref=zb.at[z], send_sem=zs, recv_sem=zr,
            device_id=(br, seg, lax.rem(z + d, TP)), device_id_type=MESH)

    for d in range(1, TP):
        zsend(d).start()
    pltpu.make_async_copy(zo, zb.at[z], zr).start()
    pltpu.make_async_copy(zb, zb, zr).wait()
    total = zb[0, :BR, :ROWS]
    for k in range(1, TP):
        total = total + zb[k, :BR, :ROWS]
    out_ref[...] = total

    pltpu.make_async_copy(tb.at[pl.ds(0, 31)], tb.at[pl.ds(0, 31)], ts).wait()
    pltpu.make_async_copy(zb.at[pl.ds(0, 15)], zb.at[pl.ds(0, 15)], zs).wait()

    @pl.when(source)
    def _():
        for d in range(SEG):
            for o in range(2):
                if d or o:
                    dist(d, o).wait_send()
    for o in range(1, BR):
        hw_send(o).wait_send()
    for k in range(2):
        to_sib(core + 2 * k, k).wait_send()
    for e in range(2):
        @pl.when(2 * lax.rem(z, 8) + e != z)
        def _():
            kv_send(e).wait_send()

    def drain(t, _):
        for h in range(2):
            @pl.when(jnp.logical_or(t < 7, jnp.logical_and(t < 8, core == 0)))
            def _():
                ring(z, t, h).wait_send()

            @pl.when(jnp.logical_and(t > 0, jnp.logical_or(t < 8, core == 0)))
            def _():
                side(z, t, h).wait_send()
        for d in range(1, SEG):
            psend(t, d, 0).wait_send()
        return 0

    lax.fori_loop(0, 9, drain, 0)


def local(rollout, send_rows, seq_lengths, attn_gain, w_query, w_keyval, head_weight, head_attn):
    sr = send_rows.reshape(SEG, PIECE)
    order = jnp.concatenate([sr[:, :8].reshape(64), sr[:, 8]])
    orow = jnp.pad(order, (0, LANES - ROWS), constant_values=-1).reshape(1, LANES)
    vm = pl.BlockSpec(memory_space=pltpu.VMEM)
    sm = pl.BlockSpec(memory_space=pltpu.SMEM)
    hbm = pl.BlockSpec(memory_space=pltpu.HBM)
    bf, f32, dma = jnp.bfloat16, jnp.float32, pltpu.SemaphoreType.DMA
    return pl.pallas_call(
        kernel,
        name="scores",
        out_shape=jax.ShapeDtypeStruct((BR, ROWS), f32),
        in_specs=[vm, vm, sm] + [hbm] * 6,
        out_specs=vm,
        scratch_shapes=[
            pltpu.VMEM((ROWS, D), bf), pltpu.VMEM((1, D), bf), pltpu.VMEM((KS, QC), bf), pltpu.VMEM((KS, KC), bf),
            pltpu.VMEM((1, QC), bf), pltpu.VMEM((1, QC), bf),
            pltpu.VMEM((2 * SEG, MSG, HK), bf),
            pltpu.VMEM((TP, BR, MSG, HK), bf),
            pltpu.VMEM((BR, PIECE, 8, CC), f32),
            pltpu.VMEM((9, 7, 32, CC), bf),
            pltpu.VMEM((7, 9, 32, CC), bf),
            pltpu.VMEM((CC // LANES, 256, LANES), f32),
            pltpu.VMEM((9, 32, CC), f32),
            pltpu.VMEM((PACK, QC), bf), pltpu.VMEM((PACK, KC), bf), pltpu.VMEM((2, PACK, KC), bf),
            pltpu.VMEM((1, QC), f32), pltpu.VMEM((BR, 1, QC), f32),
            pltpu.VMEM((PACK, PACK), f32),
            pltpu.VMEM((32, 1, LANES), f32), pltpu.VMEM((32, 1, LANES), f32),
            pltpu.VMEM((8, LANES), f32), pltpu.VMEM((TP, 8, LANES), f32),
            dma((6,)), dma((TP, BR)), dma((16,)), dma((2,)), dma((9, 2)), dma((9, 2)), dma((9, 7)), dma((7, 9)),
            dma((3,)), dma((BR,)), dma((2,)), dma((2,)), dma, dma, dma, dma,
        ],
        compiler_params=pltpu.CompilerParams(
            collective_id=0, has_side_effects=True, vmem_limit_bytes=56 << 20),
    )(order.reshape(ROWS, 1), orow, seq_lengths, rollout, attn_gain, w_query[0], w_keyval[0], head_weight, head_attn)


def solution(mesh):
    return jax.shard_map(
        local,
        mesh=mesh,
        in_specs=(
            P(("branch", "segment"), None),
            P(("branch", "segment")),
            P("segment", None),
            P("branch", None),
            P("branch", "segment", "tp"),
            P("branch", "segment", "tp"),
            P("branch", "tp"),
            P("branch", "tp"),
        ),
        out_specs=P(None, ("branch", "segment")),
        check_vma=False,
    )
```

time: 388 us -> 117 us (0.30)
  waiting for transfers between devices: 223 us -> 0 us
  Pallas kernels: 0 us -> 114 us
  blocking collectives: 79.7 us -> 0 us
  local copies, waits for them, and re-layouts: 25.2 us -> 3.47 us
  other arithmetic: 17.7 us -> 0.15 us
  matrix products: 17 us -> 0 us
  between operations: 13.3 us -> 0.01 us
  starting transfers between devices: 11.9 us -> 0 us
    all_to_all x1 -> x0, waiting for transfers between devices: 145 us -> none  [local(): lax.all_to_all(copies, ('branch', 'segment'), split_axis=0, concat_axis=0...]
    pallas_call x0 -> x1, Pallas kernels: none -> 114 us  [local(): pl.pallas_call(kernel, name='scores', out_shape=jax.ShapeDtypeStruct((BR,...]
    all_gather x3 -> x0, waiting for transfers between devices: 76.5 us -> none  [the longest x1 58.6 us: local(): keyval = lax.all_gather(keyval_part, 'tp', axis=1, tiled=True)]
    psum x1 -> x0, blocking collectives: 40.6 us -> none  [local(): totals = lax.psum(direct + through, 'tp')]
    all_to_all x1 -> x0, blocking collectives: 39.1 us -> none  [local(): lax.all_to_all(outgoing, ('branch', 'segment'), split_axis=0, concat_axis...]
    dot_general x6 -> x0, matrix products: 17 us -> none  [the longest x1 7.41 us: local(): jnp.dot(normed, lax.all_gather(w_query, 'segment', axis=1, tiled=True)[0]...]
    all_to_all x1 -> x0, starting transfers between devices: 11.6 us -> none  [local(): lax.all_to_all(copies, ('branch', 'segment'), split_axis=0, concat_axis=0...]
    convert_element_type x1 -> x0, other arithmetic: 9.94 us -> none  [local(): normed = (rows_float * lax.rsqrt(mean_square + epsilon) * attn_gain[0].as...]
  transfers between devices with their start and end apart: 4 -> 0, of which waited for: 3 -> 0; matrix products, arithmetic and copies ran while one was open for 14% -> 0% of each run, Pallas kernels for 0% -> 0%
where the time goes in v1:
time: 117 us
  Pallas kernels  114 us (97%)
  local copies, waits for them, and re-layouts  3.47 us (3%)
    pallas_call x1, Pallas kernels, local(): pl.pallas_call(kernel, name='scores', out_shape=jax.ShapeDtypeStruct((BR,...  114 us

profile of v1, /device:TPU:1, one launch (start us, length us, event | category | flops | bytes accessed | tf_op | source)
XLA Modules:
  0.0 117.2 jit_solution(3962087703207846395)
XLA Ops:
  0.0 0.7 reshape.12
  0.7 0.1 reshape.13
  0.8 0.2 slice_reduce_fusion
  1.0 0.1 fusion
  1.1 0.1 pad_add_fusion
  1.1 0.5 pad_bitcast_fusion.orow_ref
  1.7 0.7 copy.10.order_ref
  2.4 113.6 %scores.1 = f32[4,72]{1,0:T(4,128)} custom-call(s32[72,1]{1,0:T(8,128)} %copy.10.order_ref, s32[1,128]{1,0:T(1,128)} %pad_bitcast_fusion.orow_ref, s32[1,6]{1,0:T(1,128)} %len_ref.1, bf16[72,8192]{1,0:T(8,128)(2,1)} %roll_hbm.1, bf16[1,8192]{1,0:T(2,128)(2,1)} %gain_hbm.1, bf16[1024,512]{1,0:T(8,128)(2,1)} %bitcast.7, bf16[1024,128]{1,0:T(8,128)(2,1)} %bitcast.8, ...), custom_call_target="tpu_custom_call" | custom-call | tf_op jit(solution)/shard_map/scores/pallas_call | solution.py:391
  116.0 1.2 %copy.12 = f32[4,72]{1,0:T(4,128)} copy(f32[4,72]{1,0:T(4,128)} %scores.1) | data formatting | bytes 2304

commit v2 on v0

v2 whole, which is shorter than its diff:
```python
import math

import jax
import jax.numpy as jnp
from jax import lax
from jax.experimental import pallas as pl
from jax.experimental.pallas import tpu as pltpu
from jax.sharding import PartitionSpec as P

EPS = 1e-05
MESH = pl.DeviceIdType.MESH

BR, SEG, TP = 4, 8, 16
NX = 4
ROWS = 72
PIECE = 9
PACK = 288
HALF = PACK // 2
D = 8192
KS = D // SEG
HK = KS // 2
LANES = 128
HEADS_HERE = 4
CHUNKS = HEADS_HERE + 1
MSG = 80
WIDTH = HEADS_HERE * LANES


def kernel(send_ref, len_ref, roll_hbm, gain_hbm, wq_hbm, wkv_hbm, hw_hbm, ha_hbm, out_ref,
           roll, gain_v, wA, hw_v, ha_v, y, X, N, pf, pbuf, rbuf, fown, ybuf, qf, kvb, hwf, hwb, bias, tb, rb, zo, zb,
           ld, lw, xo, xz, so, sd, sl, fo, fz, rs, sf, ws, wr, ps, pr, ys, yr, hs, hr, kvs, kvr, ts, tr, zs, zr):
    f32, bf, i32 = jnp.float32, jnp.bfloat16, jnp.int32
    br = lax.axis_index("branch")
    seg = lax.axis_index("segment")
    z = lax.axis_index("tp")
    core, yh = lax.rem(br, 2), br // 2
    x, yl = lax.rem(seg, NX), seg // NX
    sib = br + 1 - 2 * core
    far = lax.rem(br + 2, BR)
    part_seg = lax.rem(seg + NX, SEG)
    step_z = 1 - 2 * core
    nxt = lax.rem(z + step_z + TP, TP)
    source = x == z // NX

    def xpeer(d):
        return yl * NX + lax.rem(x + d, NX)

    ld_roll = pltpu.make_async_copy(roll_hbm, roll, ld.at[0])
    ld_gain = pltpu.make_async_copy(gain_hbm, gain_v, ld.at[1])
    ld_hw = pltpu.make_async_copy(hw_hbm, hw_v, ld.at[2])
    ld_ha = pltpu.make_async_copy(ha_hbm, ha_v, ld.at[3])
    ld_w = [pltpu.make_async_copy(wkv_hbm, wA.at[yl, 0], lw.at[0])]
    for c in range(HEADS_HERE):
        ld_w.append(pltpu.make_async_copy(wq_hbm.at[:, pl.ds(c * LANES, LANES)], wA.at[yl, c + 1], lw.at[c + 1]))
    for c in [ld_roll, ld_hw, ld_gain] + ld_w + [ld_ha]:
        c.start()

    barrier = pltpu.get_barrier_semaphore()

    def greet(dev):
        pl.semaphore_signal(barrier, inc=1, device_id=dev, device_id_type=MESH)

    for d in range(1, NX):
        greet((br, xpeer(d), z))
    for d in range(NX):
        greet((far, xpeer(d), z))
    greet((br, part_seg, z))
    greet((sib, seg, z))
    greet((lax.rem(sib + 2, BR), seg, z))
    greet((br, seg, lax.rem(z + 1, TP)))
    greet((br, seg, lax.rem(z + TP - 1, TP)))

    drains = []

    def finish():
        for f in drains:
            f()

    sub = lax.broadcasted_iota(i32, (ROWS, LANES), 0)
    lane = lax.broadcasted_iota(i32, (ROWS, LANES), 1)
    diag = sub == lane
    src = jnp.where(sub < 64, (sub >> 3) * PIECE + (sub & 7), (sub - 64) * PIECE + 8)
    send = jnp.concatenate([send_ref[...].astype(f32), jnp.zeros((1, LANES - ROWS), f32)], axis=1)
    order = jnp.sum(jnp.where(lane == src, send, 0.0), axis=1, keepdims=True)
    order_i = order.astype(i32)
    order_row = jnp.sum(jnp.where(diag, order, 0.0), axis=0, keepdims=True).astype(i32)

    ld_roll.wait()
    xf = roll[...].astype(f32)
    r = lax.rsqrt(jnp.sum(xf * xf, axis=-1, keepdims=True) * (1.0 / D) + EPS)
    r_row = jnp.sum(jnp.where((order_row == sub) & (lane < ROWS), r, 0.0), axis=0, keepdims=True)
    hi = r_row.astype(bf).astype(f32)
    mid = (r_row - hi).astype(bf).astype(f32)
    lo = r_row - hi - mid
    s8 = lax.broadcasted_iota(i32, (8, LANES), 0)
    tail = jnp.where(s8 == 0, hi, jnp.where(s8 == 1, mid, jnp.where(s8 == 2, lo, 0.0)))
    tail = jnp.concatenate([tail] + [jnp.zeros((8, LANES), f32)] * (HK // LANES - 1), axis=1)
    perm = (order_i == lane[:, :ROWS]).astype(f32).astype(bf)
    for c in range(2 * SEG):
        yc = jnp.dot(perm, roll[:, c * HK:(c + 1) * HK], preferred_element_type=f32)
        y[c] = jnp.concatenate([yc, tail], axis=0).astype(bf)
    ld_hw.wait()
    hwf[...] = hw_v[...].astype(f32)
    for c in ld_w:
        c.wait()
    ld_gain.wait()
    ld_ha.wait()

    pl.semaphore_wait(barrier, 12)

    quarter = lax.rem(z, NX)

    def dist(d):
        xd = lax.rem(x + d, NX)
        return pltpu.make_async_remote_copy(
            src_ref=y.at[(quarter // 2) * SEG + 2 * xd + lax.rem(quarter, 2)], dst_ref=X.at[yh, z, core],
            send_sem=sd.at[d], recv_sem=xz.at[z, core], device_id=(far, yl * NX + xd, z), device_id_type=MESH)

    @pl.when(source)
    def _():
        for d in range(NX):
            dist(d).start()

    def wsend(c):
        return pltpu.make_async_remote_copy(
            src_ref=wA.at[yl, c], dst_ref=wA.at[yl, c], send_sem=ws.at[c], recv_sem=wr.at[c],
            device_id=(br, part_seg, z), device_id_type=MESH)

    for c in range(CHUNKS):
        wsend(c).start()

    def row_send(d, q):
        xd = lax.rem(x + d, NX)
        return pltpu.make_async_remote_copy(
            src_ref=y.at[pl.ds(q * SEG + 2 * xd, 2)], dst_ref=X.at[yh, pl.ds(x * NX + 2 * q, 2), core],
            send_sem=so.at[d, q], recv_sem=xo.at[x, core, q], device_id=(br, yl * NX + xd, z), device_id_type=MESH)

    def row_keep(q):
        return pltpu.make_async_copy(
            y.at[pl.ds(q * SEG + 2 * x, 2)], X.at[yh, pl.ds(x * NX + 2 * q, 2), core], xo.at[x, core, q])

    def row_side(d, q, src_ref):
        xs = lax.rem(x + d, NX)
        dst = X.at[yh, pl.ds(xs * NX + 2 * q, 2), core]
        return pltpu.make_async_remote_copy(
            src_ref=dst if src_ref is None else src_ref, dst_ref=dst, send_sem=fo.at[d, q],
            recv_sem=xo.at[xs, core, q], device_id=(sib, seg, z), device_id_type=MESH)

    def row_wait(d, q, c):
        xs = lax.rem(x + d, NX)
        ref = X.at[yh, pl.ds(xs * NX + 2 * q, 2), c]
        pltpu.make_async_copy(ref, ref, xo.at[xs, c, q]).wait()

    for d in (1, 3, 2):
        for q in range(2):
            row_send(d, q).start()
    for q in range(2):
        row_keep(q).start()
        row_side(0, q, y.at[pl.ds(q * SEG + 2 * x, 2)]).start()

    def hw_send(o):
        return pltpu.make_async_remote_copy(
            src_ref=hwf, dst_ref=hwb.at[br], send_sem=hs.at[o - 1], recv_sem=hr.at[br],
            device_id=(lax.rem(br + o, BR), seg, z), device_id_type=MESH)

    for o in range(1, BR):
        hw_send(o).start()

    @drains.append
    def _():
        @pl.when(source)
        def _():
            for d in range(NX):
                dist(d).wait_send()
        for c in range(CHUNKS):
            wsend(c).wait_send()
        for d in range(1, NX):
            for q in range(2):
                row_send(d, q).wait_send()
        for q in range(2):
            row_side(0, q, y.at[pl.ds(q * SEG + 2 * x, 2)]).wait_send()
        for o in range(1, BR):
            hw_send(o).wait_send()

    rq = lax.broadcasted_iota(i32, (PACK, PACK), 0)
    rk = lax.broadcasted_iota(i32, (PACK, PACK), 1)

    def position(p):
        low = (p >= HALF).astype(i32)
        u = p - low * HALF
        left = u >= 2 * BR * 16
        sh = jnp.where(left, u - 128, u >> 3)
        i = jnp.where(left, 8, u & 7)
        g = ((sh >> 3) * 2 + (sh & 1)) * SEG + low * NX + ((sh >> 1) & 3)
        return g * PIECE + i

    pq, pk = position(rq), position(rk)
    start = jnp.zeros((PACK, PACK), i32)
    end = jnp.int32(0)
    for e in range(len_ref.shape[1]):
        end = end + len_ref[0, e]
        start = jnp.where(pq >= end, end, start)
    bias[...] = jnp.where((pk >= start) & (pk <= pq), 0.0, -1e30)

    other = 1 - yh

    def zpiece(c):
        ref = X.at[other, z, c]
        return pltpu.make_async_copy(ref, ref, xz.at[z, c])

    def to_sib():
        return pltpu.make_async_remote_copy(
            src_ref=X.at[other, z, core], dst_ref=X.at[other, z, core], send_sem=fz, recv_sem=xz.at[z, core],
            device_id=(sib, seg, z), device_id_type=MESH)

    def ring(blk, t, h):
        return pltpu.make_async_remote_copy(
            src_ref=X.at[other, blk, h], dst_ref=X.at[other, blk, h], send_sem=rs.at[t, h],
            recv_sem=xz.at[blk, h], device_id=(br, seg, nxt), device_id_type=MESH)

    def side(blk, t, h):
        return pltpu.make_async_remote_copy(
            src_ref=X.at[other, blk, h], dst_ref=X.at[other, blk, h], send_sem=sf.at[t, h],
            recv_sem=xz.at[blk, h], device_id=(sib, seg, z), device_id_type=MESH)

    zpiece(core).wait()
    to_sib().start()
    ring(z, 0, core).start()
    zpiece(1 - core).wait()
    ring(z, 0, 1 - core).start()

    def step(t, _):
        mine = lax.rem(z - step_z * t + TP, TP)
        has = jnp.logical_or(t < 8, core == 0)
        fwd = jnp.logical_or(t < 7, jnp.logical_and(t < 8, core == 0))
        for k in range(2):
            h = lax.rem(core + k + TP, 2)

            @pl.when(has)
            def _():
                ring(mine, t, h).wait_recv()

            @pl.when(fwd)
            def _():
                ring(mine, t, h).start()

            @pl.when(has)
            def _():
                side(mine, t, h).start()
        return 0

    lax.fori_loop(1, 6, step, 0)
    for d in (1, 3):
        for q in range(2):
            row_wait(d, q, core)
            row_side(d, q, None).start()
    lax.fori_loop(6, 9, step, 0)
    for q in range(2):
        row_wait(2, q, core)
        row_side(2, q, None).start()

    @drains.append
    def _():
        to_sib().wait_send()
        for d in range(1, NX):
            for q in range(2):
                row_side(d, q, None).wait_send()

        def drain(t, _):
            for h in range(2):
                @pl.when(jnp.logical_or(t < 7, jnp.logical_and(t < 8, core == 0)))
                def _():
                    ring(z, t, h).wait_send()

                @pl.when(jnp.logical_and(t > 0, jnp.logical_or(t < 8, core == 0)))
                def _():
                    side(z, t, h).wait_send()
            return 0

        lax.fori_loop(0, 9, drain, 0)

    for d in range(NX):
        for q in range(2):
            row_wait(d, q, 1 - core)
    for q in range(2):
        row_wait(0, q, core)

    def side_wait(t, _):
        their = lax.rem(z + step_z * t + TP, TP)

        @pl.when(jnp.logical_or(t < 8, core == 1))
        def _():
            for h in range(2):
                side(their, t, h).wait_recv()
        return 0

    lax.fori_loop(1, 9, side_wait, 0)

    def norm(g, _):
        gy, gx = g // NX, lax.rem(g, NX)
        scale = []
        for c in range(2):
            row = jnp.sum(X[gy, gx * NX, c][ROWS:, :LANES].astype(f32), axis=0, keepdims=True)
            scale.append(jnp.sum(jnp.where(diag, row, 0.0), axis=-1, keepdims=True))
        for q in range(4):
            g0 = pl.multiple_of(((q // 2) * NX + x) * KS + (q % 2) * HK, HK)
            gain = gain_v[:, pl.ds(g0, HK)].astype(f32)
            v = jnp.concatenate([X[gy, gx * NX + q, c].astype(f32)[:ROWS] * scale[c] for c in range(2)], axis=0)
            N[g, :, q * HK:(q + 1) * HK] = (v * gain).astype(bf)
        return 0

    lax.fori_loop(0, 2 * NX, norm, 0)

    def psend(c, d):
        return pltpu.make_async_remote_copy(
            src_ref=pbuf.at[c, d - 1], dst_ref=rbuf.at[c, d - 1], send_sem=ps.at[c, d - 1], recv_sem=pr.at[c, d - 1],
            device_id=(br, xpeer(d), z), device_id_type=MESH)

    def ysend(c):
        return pltpu.make_async_remote_copy(
            src_ref=ybuf.at[c], dst_ref=qf.at[c, yl], send_sem=ys.at[c], recv_sem=yr.at[c],
            device_id=(br, part_seg, z), device_id_type=MESH)

    def produce(c):
        wsend(c).wait_recv()
        lhs = N[...].reshape(8 * HALF, 2 * KS)
        acc = jnp.dot(lhs[:, :KS], wA[0, c], preferred_element_type=f32)
        acc = acc + jnp.dot(lhs[:, KS:], wA[1, c], preferred_element_type=f32)
        pf[...] = acc.reshape(16, PIECE, 8, LANES)
        left = pf[:, 8].reshape(128, LANES)
        lx = lax.broadcasted_iota(i32, (16, 8, LANES), 1)
        left = left.reshape(16, 8, LANES)
        for d in range(NX):
            xd = lax.rem(x + d, NX)
            for k in range(2):
                s = k * NX + xd
                main = pf[:, s].reshape(128, LANES)
                tail = jnp.sum(jnp.where(lx == s, left, 0.0), axis=1)
                v = jnp.concatenate([main, tail], axis=0)
                if d == 0:
                    fown[c, k] = v
                else:
                    pbuf[c, d - 1, k] = v.astype(bf)
            if d:
                psend(c, d).start()

    def consume(c):
        tot = fown[c]
        for d in range(1, NX):
            psend(c, d).wait_recv()
            tot = tot + rbuf[c, d - 1].astype(f32)
        fown[c] = tot
        ybuf[c] = fown[c, 1 - yl].astype(bf)
        ysend(c).start()
        qf[c, yl] = fown[c, yl].astype(bf)

    slot = z // 8

    def kv_send(e):
        return pltpu.make_async_remote_copy(
            src_ref=qf.at[0], dst_ref=kvb.at[slot], send_sem=kvs.at[e], recv_sem=kvr.at[slot],
            device_id=(br, seg, 2 * lax.rem(z, 8) + e), device_id_type=MESH)

    keep = pltpu.make_async_copy(qf.at[0], kvb.at[slot], kvr.at[slot])

    def kv_start():
        ysend(0).wait_recv()
        for e in range(2):
            here = 2 * lax.rem(z, 8) + e == z

            @pl.when(here)
            def _():
                keep.start()

            @pl.when(jnp.logical_not(here))
            def _():
                kv_send(e).start()

    def chunk(c, _):
        produce(c)

        @pl.when(c > 0)
        def _():
            consume(c - 1)

        @pl.when(c == 2)
        def _():
            kv_start()
        return 0

    lax.fori_loop(0, CHUNKS, chunk, 0)

    @drains.append
    def _():
        def drain(c, _):
            for d in range(1, NX):
                psend(c, d).wait_send()
            ysend(c).wait_send()
            return 0

        lax.fori_loop(0, CHUNKS, drain, 0)
        for e in range(2):
            @pl.when(2 * lax.rem(z, 8) + e != z)
            def _():
                kv_send(e).wait_send()

    for o in range(1, BR):
        frm = lax.rem(br + o, BR)
        pltpu.make_async_copy(hwb.at[frm], hwb.at[frm], hr.at[frm]).wait()
    hwb[br] = hwf[...]
    hw4 = jnp.concatenate([hwb[m] for m in range(BR)] + [jnp.zeros((4, WIDTH), f32)], axis=0).astype(bf)
    c0 = pl.multiple_of(z * WIDTH, WIDTH)
    direct = lax.dot_general(hw4, roll[:, pl.ds(c0, WIDTH)], (((1,), (1,)), ((), ())), preferred_element_type=f32)
    lanes16 = lax.broadcasted_iota(i32, (16, LANES), 1)
    table = jnp.concatenate(
        [jnp.concatenate([order_i[s * 8:(s + 1) * 8], order_i[64:72]], axis=0) == lanes16 for s in range(SEG)], axis=1)
    table = table.astype(f32).astype(bf)

    consume(CHUNKS - 1)
    for k in range(2):
        pltpu.make_async_copy(kvb.at[k], kvb.at[k], kvr.at[k]).wait()
    keys, values = kvb[0].reshape(PACK, LANES), kvb[1].reshape(PACK, LANES)
    acc = jnp.zeros((PACK, LANES), f32)
    for h in range(HEADS_HERE):
        ysend(h + 1).wait_recv()
        logits = lax.dot_general(qf[h + 1].reshape(PACK, LANES), keys, (((1,), (1,)), ((), ())),
                                 preferred_element_type=f32)
        logits = logits * (1.0 / math.sqrt(LANES)) + bias[...]
        expo = jnp.exp(logits - jnp.max(logits, axis=-1, keepdims=True))
        probs = (expo * (1.0 / jnp.sum(expo, axis=-1, keepdims=True))).astype(bf)
        att = jnp.dot(probs, values, preferred_element_type=f32)
        acc = acc + att * ha_v[:, h * LANES:(h + 1) * LANES].astype(f32)
    through = jnp.sum(acc, axis=-1, keepdims=True)
    sub = lax.broadcasted_iota(i32, (128, LANES), 0)
    lane = lax.broadcasted_iota(i32, (128, LANES), 1)
    for k in range(2):
        rows = through[k * HALF:(k + 1) * HALF]
        main = jnp.where((sub & 7) == lane, rows[:128], 0.0).reshape(16, 8, LANES).sum(axis=1)
        main = main + jnp.where(lane[:16] == 8 + seg, rows[128:], 0.0)
        tb[k * 16:(k + 1) * 16] = main.reshape(16, 1, LANES)

    def at(b2, s2):
        return (s2 // NX) * 16 + ((b2 // 2) * NX + lax.rem(s2, NX)) * 2 + lax.rem(b2, 2)

    def tsend(o, d):
        b2, s2 = lax.rem(br + o, BR), lax.rem(seg + d, SEG)
        return pltpu.make_async_remote_copy(
            src_ref=tb.at[at(b2, s2)], dst_ref=rb.at[br * SEG + seg], send_sem=ts, recv_sem=tr,
            device_id=(b2, s2, z), device_id_type=MESH)

    for o in range(BR):
        for d in range(SEG):
            if o or d:
                tsend(o, d).start()
    pltpu.make_async_copy(tb.at[at(br, seg)], rb.at[br * SEG + seg], tr).start()
    pltpu.make_async_copy(rb, rb, tr).wait()

    @drains.append
    def _():
        pltpu.make_async_copy(tb.at[pl.ds(0, 31)], tb.at[pl.ds(0, 31)], ts).wait()

    got = rb[...].reshape(32, LANES)[:, :16]
    g_hi = got.astype(bf)
    rest = got - g_hi.astype(f32)
    g_mid = rest.astype(bf)
    g_lo = (rest - g_mid.astype(f32)).astype(bf)
    routed = jnp.dot(g_hi, table, preferred_element_type=f32)
    routed = routed + jnp.dot(g_mid, table, preferred_element_type=f32)
    routed = routed + jnp.dot(g_lo, table, preferred_element_type=f32)
    pack_of = lax.broadcasted_iota(i32, (32, LANES), 0) & 7
    part = jnp.zeros((32, LANES), f32)
    for s in range(SEG):
        part = part + jnp.where(pack_of == s, routed[:, s * LANES:(s + 1) * LANES], 0.0)
    part = part.reshape(BR, SEG, LANES).sum(axis=1)
    zo[...] = jnp.zeros((BR, LANES), f32)
    zo[:, :ROWS] = part[:, :ROWS] + direct[:BR]

    def zsend(d):
        return pltpu.make_async_remote_copy(
            src_ref=zo, dst_ref=zb.at[z], send_sem=zs, recv_sem=zr,
            device_id=(br, seg, lax.rem(z + d, TP)), device_id_type=MESH)

    for d in range(1, TP):
        zsend(d).start()
    pltpu.make_async_copy(zo, zb.at[z], zr).start()
    pltpu.make_async_copy(zb, zb, zr).wait()

    @drains.append
    def _():
        pltpu.make_async_copy(zb.at[pl.ds(0, 15)], zb.at[pl.ds(0, 15)], zs).wait()

    total = zb[0, :, :ROWS]
    for k in range(1, TP):
        total = total + zb[k, :, :ROWS]
    out_ref[...] = total
    finish()


def local(rollout, send_rows, seq_lengths, attn_gain, w_query, w_keyval, head_weight, head_attn):
    vm = pl.BlockSpec(memory_space=pltpu.VMEM)
    sm = pl.BlockSpec(memory_space=pltpu.SMEM)
    hbm = pl.BlockSpec(memory_space=pltpu.HBM)
    bf, f32, dma = jnp.bfloat16, jnp.float32, pltpu.SemaphoreType.DMA
    return pl.pallas_call(
        kernel,
        name="scores",
        out_shape=jax.ShapeDtypeStruct((BR, ROWS), f32),
        in_specs=[vm, sm] + [hbm] * 6,
        out_specs=vm,
        scratch_shapes=[
            pltpu.VMEM((ROWS, D), bf), pltpu.VMEM((1, D), bf), pltpu.VMEM((2, CHUNKS, KS, LANES), bf),
            pltpu.VMEM((1, WIDTH), bf), pltpu.VMEM((1, WIDTH), bf),
            pltpu.VMEM((2 * SEG, MSG, HK), bf),
            pltpu.VMEM((2, TP, 2, MSG, HK), bf),
            pltpu.VMEM((8, HALF, 2 * KS), bf),
            pltpu.VMEM((16, PIECE, 8, LANES), f32),
            pltpu.VMEM((CHUNKS, 3, 2, HALF, LANES), bf),
            pltpu.VMEM((CHUNKS, 3, 2, HALF, LANES), bf),
            pltpu.VMEM((CHUNKS, 2, HALF, LANES), f32),
            pltpu.VMEM((CHUNKS, HALF, LANES), bf),
            pltpu.VMEM((CHUNKS, 2, HALF, LANES), bf),
            pltpu.VMEM((2, 2, HALF, LANES), bf),
            pltpu.VMEM((1, WIDTH), f32), pltpu.VMEM((BR, 1, WIDTH), f32),
            pltpu.VMEM((PACK, PACK), f32),
            pltpu.VMEM((32, 1, LANES), f32), pltpu.VMEM((32, 1, LANES), f32),
            pltpu.VMEM((BR, LANES), f32), pltpu.VMEM((TP, BR, LANES), f32),
            dma((4,)), dma((CHUNKS,)), dma((NX, 2, 2)), dma((TP, 2)), dma((NX, 2)), dma((NX,)), dma((2,)),
            dma((NX, 2)), dma, dma((9, 2)), dma((9, 2)), dma((CHUNKS,)), dma((CHUNKS,)),
            dma((CHUNKS, 3)), dma((CHUNKS, 3)), dma((CHUNKS,)), dma((CHUNKS,)),
            dma((3,)), dma((BR,)), dma((2,)), dma((2,)), dma, dma, dma, dma,
        ],
        compiler_params=pltpu.CompilerParams(
            collective_id=0, has_side_effects=True, vmem_limit_bytes=56 << 20),
    )(send_rows.reshape(1, ROWS), seq_lengths, rollout, attn_gain, w_query[0], w_keyval[0], head_weight, head_attn)


def solution(mesh):
    return jax.shard_map(
        local,
        mesh=mesh,
        in_specs=(
            P(("branch", "segment"), None),
            P(("branch", "segment")),
            P("segment", None),
            P("branch", None),
            P("branch", "segment", "tp"),
            P("branch", "segment", "tp"),
            P("branch", "tp"),
            P("branch", "tp"),
        ),
        out_specs=P(None, ("branch", "segment")),
        check_vma=False,
    )
```

time: 388 us -> 95.7 us (0.25)
  waiting for transfers between devices: 223 us -> 0 us
  Pallas kernels: 0 us -> 94.2 us
  blocking collectives: 79.7 us -> 0 us
  local copies, waits for them, and re-layouts: 25.2 us -> 1.26 us
  other arithmetic: 17.7 us -> 0 us
  matrix products: 17 us -> 0 us
  between operations: 13.3 us -> 0.01 us
  starting transfers between devices: 11.9 us -> 0 us
    all_to_all x1 -> x0, waiting for transfers between devices: 145 us -> none  [local(): lax.all_to_all(copies, ('branch', 'segment'), split_axis=0, concat_axis=0...]
    pallas_call x0 -> x1, Pallas kernels: none -> 94.2 us  [local(): pl.pallas_call(kernel, name='scores', out_shape=jax.ShapeDtypeStruct((BR,...]
    all_gather x3 -> x0, waiting for transfers between devices: 76.5 us -> none  [the longest x1 58.6 us: local(): keyval = lax.all_gather(keyval_part, 'tp', axis=1, tiled=True)]
    psum x1 -> x0, blocking collectives: 40.6 us -> none  [local(): totals = lax.psum(direct + through, 'tp')]
    all_to_all x1 -> x0, blocking collectives: 39.1 us -> none  [local(): lax.all_to_all(outgoing, ('branch', 'segment'), split_axis=0, concat_axis...]
    dot_general x6 -> x0, matrix products: 17 us -> none  [the longest x1 7.41 us: local(): jnp.dot(normed, lax.all_gather(w_query, 'segment', axis=1, tiled=True)[0]...]
    all_to_all x1 -> x0, starting transfers between devices: 11.6 us -> none  [local(): lax.all_to_all(copies, ('branch', 'segment'), split_axis=0, concat_axis=0...]
    convert_element_type x1 -> x0, other arithmetic: 9.94 us -> none  [local(): normed = (rows_float * lax.rsqrt(mean_square + epsilon) * attn_gain[0].as...]
  transfers between devices with their start and end apart: 4 -> 0, of which waited for: 3 -> 0; matrix products, arithmetic and copies ran while one was open for 14% -> 0% of each run, Pallas kernels for 0% -> 0%
where the time goes in v2:
time: 95.7 us; the launch traced here: 95.5 us
  Pallas kernels  94.2 us (98%)
  local copies, waits for them, and re-layouts  1.26 us (1%)
    pallas_call x1, Pallas kernels, local(): pl.pallas_call(kernel, name='scores', out_shape=jax.ShapeDtypeStruct((BR,...  94.2 us

profile of v2, /device:TPU:1, one launch (start us, length us, event | category | flops | bytes accessed | tf_op | source)
XLA Modules:
  0.0 95.5 jit_solution(10609331219234092048)
XLA Ops:
  0.0 94.2 %scores.1 = f32[4,72]{1,0:T(4,128)} custom-call(s32[1,72]{1,0:T(1,128)} %bitcast.5, s32[1,6]{1,0:T(1,128)} %len_ref.1, bf16[72,8192]{1,0:T(8,128)(2,1)} %roll_hbm.1, bf16[1,8192]{1,0:T(2,128)(2,1)} %gain_hbm.1, bf16[1024,512]{1,0:T(8,128)(2,1)} %bitcast.3, bf16[1024,128]{1,0:T(8,128)(2,1)} %bitcast.4, bf16[1,512]{1,0:T(2,128)(2,1)} %hw_hbm.1, ...), custom_call_target="tpu_custom_call" | custom-call | tf_op jit(solution)/shard_map/scores/pallas_call | solution.py:504
  94.2 1.3 %copy.10 = f32[4,72]{1,0:T(4,128)} copy(f32[4,72]{1,0:T(4,128)} %scores.1) | data formatting | bytes 2304

commit v3 on v2

--- a/solution.py
+++ b/solution.py
@@ -28,7 +28,7 @@
 
 def kernel(send_ref, len_ref, roll_hbm, gain_hbm, wq_hbm, wkv_hbm, hw_hbm, ha_hbm, out_ref,
            roll, gain_v, wA, hw_v, ha_v, y, X, N, pf, pbuf, rbuf, fown, ybuf, qf, kvb, hwf, hwb, bias, tb, rb, zo, zb,
-           ld, lw, xo, xz, so, sd, sl, fo, fz, rs, sf, ws, wr, ps, pr, ys, yr, hs, hr, kvs, kvr, ts, tr, zs, zr):
+           ld, lw, xo, xq, so, sd, fo, fq, zn, ws, wr, ps, pr, ys, yr, hs, hr, kvs, kvr, ts, tr, zs, zr, ra, rb4):
     f32, bf, i32 = jnp.float32, jnp.bfloat16, jnp.int32
     br = lax.axis_index("branch")
     seg = lax.axis_index("segment")
@@ -38,9 +38,7 @@
     sib = br + 1 - 2 * core
     far = lax.rem(br + 2, BR)
     part_seg = lax.rem(seg + NX, SEG)
-    step_z = 1 - 2 * core
-    nxt = lax.rem(z + step_z + TP, TP)
-    source = x == z // NX
+    quarter = lax.rem(z, NX)
 
     def xpeer(d):
         return yl * NX + lax.rem(x + d, NX)
@@ -67,8 +65,8 @@
     greet((br, part_seg, z))
     greet((sib, seg, z))
     greet((lax.rem(sib + 2, BR), seg, z))
-    greet((br, seg, lax.rem(z + 1, TP)))
-    greet((br, seg, lax.rem(z + TP - 1, TP)))
+    for d in (1, 2, TP - 2, TP - 1):
+        greet((br, seg, lax.rem(z + d, TP)))
 
     drains = []
 
@@ -106,20 +104,22 @@
     ld_gain.wait()
     ld_ha.wait()
 
-    pl.semaphore_wait(barrier, 12)
-
-    quarter = lax.rem(z, NX)
+    pl.semaphore_wait(barrier, 14)
+
+    def spread(sem, d):
+        for e in (d, TP - d):
+            pl.semaphore_signal(sem, inc=1, device_id=(br, seg, lax.rem(z + e, TP)), device_id_type=MESH)
+
+    spread(ra, 2)
 
     def dist(d):
         xd = lax.rem(x + d, NX)
         return pltpu.make_async_remote_copy(
-            src_ref=y.at[(quarter // 2) * SEG + 2 * xd + lax.rem(quarter, 2)], dst_ref=X.at[yh, z, core],
-            send_sem=sd.at[d], recv_sem=xz.at[z, core], device_id=(far, yl * NX + xd, z), device_id_type=MESH)
-
-    @pl.when(source)
-    def _():
-        for d in range(NX):
-            dist(d).start()
+            src_ref=y.at[(quarter // 2) * SEG + 2 * xd + lax.rem(quarter, 2)], dst_ref=X.at[yh, x * NX + quarter, core],
+            send_sem=sd.at[d], recv_sem=xq.at[x, quarter, core], device_id=(far, yl * NX + xd, z), device_id_type=MESH)
+
+    for d in range(NX):
+        dist(d).start()
 
     def wsend(c):
         return pltpu.make_async_remote_copy(
@@ -168,10 +168,8 @@
 
     @drains.append
     def _():
-        @pl.when(source)
-        def _():
-            for d in range(NX):
-                dist(d).wait_send()
+        for d in range(NX):
+            dist(d).wait_send()
         for c in range(CHUNKS):
             wsend(c).wait_send()
         for d in range(1, NX):
@@ -204,97 +202,65 @@
 
     other = 1 - yh
 
-    def zpiece(c):
-        ref = X.at[other, z, c]
-        return pltpu.make_async_copy(ref, ref, xz.at[z, c])
-
-    def to_sib():
-        return pltpu.make_async_remote_copy(
-            src_ref=X.at[other, z, core], dst_ref=X.at[other, z, core], send_sem=fz, recv_sem=xz.at[z, core],
+    def block(xp, q, c):
+        return X.at[other, xp * NX + q, c]
+
+    def zshare(xp, k):
+        dz = (1, TP - 1, jnp.where(lax.rem(xp, 2) == 0, 2, TP - 2))[k]
+        ref = block(xp, quarter, core)
+        return pltpu.make_async_remote_copy(
+            src_ref=ref, dst_ref=ref, send_sem=zn.at[xp, k], recv_sem=xq.at[xp, quarter, core],
+            device_id=(br, seg, lax.rem(z + dz, TP)), device_id_type=MESH)
+
+    def to_sib(xp, q):
+        ref = block(xp, q, core)
+        return pltpu.make_async_remote_copy(
+            src_ref=ref, dst_ref=ref, send_sem=fq.at[xp, q], recv_sem=xq.at[xp, q, core],
             device_id=(sib, seg, z), device_id_type=MESH)
 
-    def ring(blk, t, h):
-        return pltpu.make_async_remote_copy(
-            src_ref=X.at[other, blk, h], dst_ref=X.at[other, blk, h], send_sem=rs.at[t, h],
-            recv_sem=xz.at[blk, h], device_id=(br, seg, nxt), device_id_type=MESH)
-
-    def side(blk, t, h):
-        return pltpu.make_async_remote_copy(
-            src_ref=X.at[other, blk, h], dst_ref=X.at[other, blk, h], send_sem=sf.at[t, h],
-            recv_sem=xz.at[blk, h], device_id=(sib, seg, z), device_id_type=MESH)
-
-    zpiece(core).wait()
-    to_sib().start()
-    ring(z, 0, core).start()
-    zpiece(1 - core).wait()
-    ring(z, 0, 1 - core).start()
-
-    def step(t, _):
-        mine = lax.rem(z - step_z * t + TP, TP)
-        has = jnp.logical_or(t < 8, core == 0)
-        fwd = jnp.logical_or(t < 7, jnp.logical_and(t < 8, core == 0))
-        for k in range(2):
-            h = lax.rem(core + k + TP, 2)
-
-            @pl.when(has)
-            def _():
-                ring(mine, t, h).wait_recv()
-
-            @pl.when(fwd)
-            def _():
-                ring(mine, t, h).start()
-
-            @pl.when(has)
-            def _():
-                side(mine, t, h).start()
-        return 0
-
-    lax.fori_loop(1, 6, step, 0)
-    for d in (1, 3):
+    def block_wait(xp, q, c):
+        ref = block(xp, q, c)
+        pltpu.make_async_copy(ref, ref, xq.at[xp, q, c]).wait()
+
+    for d in (0, 1, 3, 2):
+        xp = lax.rem(x + d, NX)
+        block_wait(xp, quarter, core)
+        for k in range(3):
+            zshare(xp, k).start()
+        to_sib(xp, quarter).start()
+    pl.semaphore_wait(ra, 2)
+    spread(rb4, 4)
+
+    for d in (1, 3, 2):
         for q in range(2):
             row_wait(d, q, core)
             row_side(d, q, None).start()
-    lax.fori_loop(6, 9, step, 0)
-    for q in range(2):
-        row_wait(2, q, core)
-        row_side(2, q, None).start()
+    for d in (0, 1, 3, 2):
+        xp = lax.rem(x + d, NX)
+        for k in (1, 3, 2):
+            q = lax.rem(quarter + k, NX)
+            block_wait(xp, q, core)
+            to_sib(xp, q).start()
 
     @drains.append
     def _():
-        to_sib().wait_send()
         for d in range(1, NX):
             for q in range(2):
                 row_side(d, q, None).wait_send()
-
-        def drain(t, _):
-            for h in range(2):
-                @pl.when(jnp.logical_or(t < 7, jnp.logical_and(t < 8, core == 0)))
-                def _():
-                    ring(z, t, h).wait_send()
-
-                @pl.when(jnp.logical_and(t > 0, jnp.logical_or(t < 8, core == 0)))
-                def _():
-                    side(z, t, h).wait_send()
-            return 0
-
-        lax.fori_loop(0, 9, drain, 0)
+        for xp in range(NX):
+            for k in range(3):
+                zshare(xp, k).wait_send()
+            for q in range(4):
+                to_sib(xp, q).wait_send()
 
     for d in range(NX):
         for q in range(2):
             row_wait(d, q, 1 - core)
     for q in range(2):
         row_wait(0, q, core)
-
-    def side_wait(t, _):
-        their = lax.rem(z + step_z * t + TP, TP)
-
-        @pl.when(jnp.logical_or(t < 8, core == 1))
-        def _():
-            for h in range(2):
-                side(their, t, h).wait_recv()
-        return 0
-
-    lax.fori_loop(1, 9, side_wait, 0)
+    for xp in range(NX):
+        for q in range(4):
+            block_wait(xp, q, 1 - core)
 
     def norm(g, _):
         gy, gx = g // NX, lax.rem(g, NX)
@@ -364,6 +330,7 @@
     keep = pltpu.make_async_copy(qf.at[0], kvb.at[slot], kvr.at[slot])
 
     def kv_start():
+        pl.semaphore_wait(rb4, 2)
         ysend(0).wait_recv()
         for e in range(2):
             here = 2 * lax.rem(z, 8) + e == z
@@ -524,10 +491,11 @@
             pltpu.VMEM((PACK, PACK), f32),
             pltpu.VMEM((32, 1, LANES), f32), pltpu.VMEM((32, 1, LANES), f32),
             pltpu.VMEM((BR, LANES), f32), pltpu.VMEM((TP, BR, LANES), f32),
-            dma((4,)), dma((CHUNKS,)), dma((NX, 2, 2)), dma((TP, 2)), dma((NX, 2)), dma((NX,)), dma((2,)),
-            dma((NX, 2)), dma, dma((9, 2)), dma((9, 2)), dma((CHUNKS,)), dma((CHUNKS,)),
+            dma((4,)), dma((CHUNKS,)), dma((NX, 2, 2)), dma((NX, 4, 2)), dma((NX, 2)), dma((NX,)),
+            dma((NX, 2)), dma((NX, 4)), dma((NX, 3)), dma((CHUNKS,)), dma((CHUNKS,)),
             dma((CHUNKS, 3)), dma((CHUNKS, 3)), dma((CHUNKS,)), dma((CHUNKS,)),
             dma((3,)), dma((BR,)), dma((2,)), dma((2,)), dma, dma, dma, dma,
+            pltpu.SemaphoreType.REGULAR, pltpu.SemaphoreType.REGULAR,
         ],
         compiler_params=pltpu.CompilerParams(
             collective_id=0, has_side_effects=True, vmem_limit_bytes=56 << 20),

time: 95.7 us -> 84.7 us (0.89)
  Pallas kernels: 94.2 us -> 83.3 us
    pallas_call x1, Pallas kernels: 94.2 us -> 83.3 us  [local(): pl.pallas_call(kernel, name='scores', out_shape=jax.ShapeDtypeStruct((BR,...]
where the time goes in v3:
time: 84.7 us; the launch traced here: 84.5 us
  Pallas kernels  83.3 us (98%)
  local copies, waits for them, and re-layouts  1.26 us (1%)
    pallas_call x1, Pallas kernels, local(): pl.pallas_call(kernel, name='scores', out_shape=jax.ShapeDtypeStruct((BR,...  83.3 us

profile of v3, /device:TPU:1, one launch (start us, length us, event | category | flops | bytes accessed | tf_op | source)
XLA Modules:
  0.0 84.5 jit_solution(11975998142784449954)
XLA Ops:
  0.0 83.3 %scores.1 = f32[4,72]{1,0:T(4,128)} custom-call(s32[1,72]{1,0:T(1,128)} %bitcast.5, s32[1,6]{1,0:T(1,128)} %len_ref.1, bf16[72,8192]{1,0:T(8,128)(2,1)} %roll_hbm.1, bf16[1,8192]{1,0:T(2,128)(2,1)} %gain_hbm.1, bf16[1024,512]{1,0:T(8,128)(2,1)} %bitcast.3, bf16[1024,128]{1,0:T(8,128)(2,1)} %bitcast.4, bf16[1,512]{1,0:T(2,128)(2,1)} %hw_hbm.1, ...), custom_call_target="tpu_custom_call" | custom-call | tf_op jit(solution)/shard_map/scores/pallas_call | solution.py:471
  83.3 1.3 %copy.10 = f32[4,72]{1,0:T(4,128)} copy(f32[4,72]{1,0:T(4,128)} %scores.1) | data formatting | bytes 2304

commit v4 on v3

--- a/solution.py
+++ b/solution.py
@@ -27,7 +27,7 @@
 
 
 def kernel(send_ref, len_ref, roll_hbm, gain_hbm, wq_hbm, wkv_hbm, hw_hbm, ha_hbm, out_ref,
-           roll, gain_v, wA, hw_v, ha_v, y, X, N, pf, pbuf, rbuf, fown, ybuf, qf, kvb, hwf, hwb, bias, tb, rb, zo, zb,
+           roll, gain_v, wA, hw_v, ha_v, y, X, N, pf, lsave, pbuf, rbuf, fown, ybuf, qf, kvb, hwf, hwb, bias, tb, rb, zo, zb,
            ld, lw, xo, xq, so, sd, fo, fq, zn, ws, wr, ps, pr, ys, yr, hs, hr, kvs, kvr, ts, tr, zs, zr, ra, rb4):
     f32, bf, i32 = jnp.float32, jnp.bfloat16, jnp.int32
     br = lax.axis_index("branch")
@@ -73,6 +73,7 @@
     def finish():
         for f in drains:
             f()
+        drains.clear()
 
     sub = lax.broadcasted_iota(i32, (ROWS, LANES), 0)
     lane = lax.broadcasted_iota(i32, (ROWS, LANES), 1)
@@ -126,7 +127,11 @@
             src_ref=wA.at[yl, c], dst_ref=wA.at[yl, c], send_sem=ws.at[c], recv_sem=wr.at[c],
             device_id=(br, part_seg, z), device_id_type=MESH)
 
-    for c in range(CHUNKS):
+    def w_next(c):
+        wsend(c - 2).wait_send()
+        wsend(c).start()
+
+    for c in range(2):
         wsend(c).start()
 
     def row_send(d, q):
@@ -170,7 +175,7 @@
     def _():
         for d in range(NX):
             dist(d).wait_send()
-        for c in range(CHUNKS):
+        for c in range(CHUNKS - 2, CHUNKS):
             wsend(c).wait_send()
         for d in range(1, NX):
             for q in range(2):
@@ -186,10 +191,11 @@
     def position(p):
         low = (p >= HALF).astype(i32)
         u = p - low * HALF
-        left = u >= 2 * BR * 16
+        left = u >= 128
         sh = jnp.where(left, u - 128, u >> 3)
         i = jnp.where(left, 8, u & 7)
-        g = ((sh >> 3) * 2 + (sh & 1)) * SEG + low * NX + ((sh >> 1) & 3)
+        hi_row = jnp.where(sh >= 8, 1 - yh, yh)
+        g = (hi_row * 2 + (sh & 1)) * SEG + low * NX + ((sh >> 1) & 3)
         return g * PIECE + i
 
     pq, pk = position(rq), position(rk)
@@ -231,36 +237,12 @@
     pl.semaphore_wait(ra, 2)
     spread(rb4, 4)
 
+    w_next(2)
     for d in (1, 3, 2):
         for q in range(2):
             row_wait(d, q, core)
             row_side(d, q, None).start()
-    for d in (0, 1, 3, 2):
-        xp = lax.rem(x + d, NX)
-        for k in (1, 3, 2):
-            q = lax.rem(quarter + k, NX)
-            block_wait(xp, q, core)
-            to_sib(xp, q).start()
-
-    @drains.append
-    def _():
-        for d in range(1, NX):
-            for q in range(2):
-                row_side(d, q, None).wait_send()
-        for xp in range(NX):
-            for k in range(3):
-                zshare(xp, k).wait_send()
-            for q in range(4):
-                to_sib(xp, q).wait_send()
-
-    for d in range(NX):
-        for q in range(2):
-            row_wait(d, q, 1 - core)
-    for q in range(2):
-        row_wait(0, q, core)
-    for xp in range(NX):
-        for q in range(4):
-            block_wait(xp, q, 1 - core)
+    w_next(3)
 
     def norm(g, _):
         gy, gx = g // NX, lax.rem(g, NX)
@@ -275,51 +257,101 @@
             N[g, :, q * HK:(q + 1) * HK] = (v * gain).astype(bf)
         return 0
 
-    lax.fori_loop(0, 2 * NX, norm, 0)
-
-    def psend(c, d):
-        return pltpu.make_async_remote_copy(
-            src_ref=pbuf.at[c, d - 1], dst_ref=rbuf.at[c, d - 1], send_sem=ps.at[c, d - 1], recv_sem=pr.at[c, d - 1],
-            device_id=(br, xpeer(d), z), device_id_type=MESH)
+    def psend(c, d, part):
+        rows = pl.ds(64 * part, 64 + 16 * part)
+        return pltpu.make_async_remote_copy(
+            src_ref=pbuf.at[c, d - 1, :, rows], dst_ref=rbuf.at[c, d - 1, :, rows], send_sem=ps.at[c, d - 1, part],
+            recv_sem=pr.at[c, d - 1, part], device_id=(br, xpeer(d), z), device_id_type=MESH)
 
     def ysend(c):
         return pltpu.make_async_remote_copy(
             src_ref=ybuf.at[c], dst_ref=qf.at[c, yl], send_sem=ys.at[c], recv_sem=yr.at[c],
             device_id=(br, part_seg, z), device_id_type=MESH)
 
-    def produce(c):
-        wsend(c).wait_recv()
-        lhs = N[...].reshape(8 * HALF, 2 * KS)
+    def produce(c, part):
+        gy = yh if part == 0 else other
+        lhs = N[pl.ds(gy * NX, NX)].reshape(NX * HALF, 2 * KS)
         acc = jnp.dot(lhs[:, :KS], wA[0, c], preferred_element_type=f32)
         acc = acc + jnp.dot(lhs[:, KS:], wA[1, c], preferred_element_type=f32)
-        pf[...] = acc.reshape(16, PIECE, 8, LANES)
-        left = pf[:, 8].reshape(128, LANES)
-        lx = lax.broadcasted_iota(i32, (16, 8, LANES), 1)
-        left = left.reshape(16, 8, LANES)
+        pf[part] = acc.reshape(8, PIECE, 8, LANES)
+        left = pf[part, :, 8]
+        if part == 0:
+            lsave[c] = left
+        else:
+            left = jnp.concatenate([lsave[c], left], axis=0)
+            lx = lax.broadcasted_iota(i32, (16, 8, LANES), 1)
         for d in range(NX):
             xd = lax.rem(x + d, NX)
             for k in range(2):
                 s = k * NX + xd
-                main = pf[:, s].reshape(128, LANES)
-                tail = jnp.sum(jnp.where(lx == s, left, 0.0), axis=1)
-                v = jnp.concatenate([main, tail], axis=0)
+                v = pf[part, :, s].reshape(64, LANES)
+                if part:
+                    v = jnp.concatenate([v, jnp.sum(jnp.where(lx == s, left, 0.0), axis=1)], axis=0)
+                rows = pl.ds(64 * part, 64 + 16 * part)
                 if d == 0:
-                    fown[c, k] = v
+                    fown[c, k, rows] = v
                 else:
-                    pbuf[c, d - 1, k] = v.astype(bf)
+                    pbuf[c, d - 1, k, rows] = v.astype(bf)
             if d:
-                psend(c, d).start()
+                psend(c, d, part).start()
 
     def consume(c):
         tot = fown[c]
         for d in range(1, NX):
-            psend(c, d).wait_recv()
+            for part in range(2):
+                psend(c, d, part).wait_recv()
             tot = tot + rbuf[c, d - 1].astype(f32)
         fown[c] = tot
         ybuf[c] = fown[c, 1 - yl].astype(bf)
         ysend(c).start()
         qf[c, yl] = fown[c, yl].astype(bf)
 
+    for q in range(2):
+        row_wait(0, q, core)
+        for d in range(NX):
+            row_wait(d, q, 1 - core)
+
+    def norm_own(g, _):
+        return norm(yh * NX + g, 0)
+
+    lax.fori_loop(0, NX, norm_own, 0)
+
+    def early(c, _):
+        wsend(c).wait_recv()
+        produce(c, 0)
+        return 0
+
+    lax.fori_loop(0, 2, early, 0)
+
+    for d in (0, 1, 3, 2):
+        xp = lax.rem(x + d, NX)
+        for k in (1, 3, 2):
+            q = lax.rem(quarter + k, NX)
+            block_wait(xp, q, core)
+            to_sib(xp, q).start()
+        if d == 1:
+            w_next(4)
+
+    @drains.append
+    def _():
+        for d in range(1, NX):
+            for q in range(2):
+                row_side(d, q, None).wait_send()
+        for xp in range(NX):
+            for k in range(3):
+                zshare(xp, k).wait_send()
+            for q in range(4):
+                to_sib(xp, q).wait_send()
+
+    for xp in range(NX):
+        for q in range(4):
+            block_wait(xp, q, 1 - core)
+
+    def norm_far(g, _):
+        return norm(other * NX + g, 0)
+
+    lax.fori_loop(0, NX, norm_far, 0)
+
     slot = z // 8
 
     def kv_send(e):
@@ -344,7 +376,12 @@
                 kv_send(e).start()
 
     def chunk(c, _):
-        produce(c)
+        @pl.when(c >= 2)
+        def _():
+            wsend(c).wait_recv()
+            produce(c, 0)
+
+        produce(c, 1)
 
         @pl.when(c > 0)
         def _():
@@ -361,7 +398,8 @@
     def _():
         def drain(c, _):
             for d in range(1, NX):
-                psend(c, d).wait_send()
+                for part in range(2):
+                    psend(c, d, part).wait_send()
             ysend(c).wait_send()
             return 0
 
@@ -407,7 +445,7 @@
         tb[k * 16:(k + 1) * 16] = main.reshape(16, 1, LANES)
 
     def at(b2, s2):
-        return (s2 // NX) * 16 + ((b2 // 2) * NX + lax.rem(s2, NX)) * 2 + lax.rem(b2, 2)
+        return (s2 // NX) * 16 + jnp.where(b2 // 2 == yh, 0, 8) + lax.rem(s2, NX) * 2 + lax.rem(b2, 2)
 
     def tsend(o, d):
         b2, s2 = lax.rem(br + o, BR), lax.rem(seg + d, SEG)
@@ -420,6 +458,7 @@
             if o or d:
                 tsend(o, d).start()
     pltpu.make_async_copy(tb.at[at(br, seg)], rb.at[br * SEG + seg], tr).start()
+    finish()
     pltpu.make_async_copy(rb, rb, tr).wait()
 
     @drains.append
@@ -480,7 +519,8 @@
             pltpu.VMEM((2 * SEG, MSG, HK), bf),
             pltpu.VMEM((2, TP, 2, MSG, HK), bf),
             pltpu.VMEM((8, HALF, 2 * KS), bf),
-            pltpu.VMEM((16, PIECE, 8, LANES), f32),
+            pltpu.VMEM((2, 8, PIECE, 8, LANES), f32),
+            pltpu.VMEM((CHUNKS, 8, 8, LANES), f32),
             pltpu.VMEM((CHUNKS, 3, 2, HALF, LANES), bf),
             pltpu.VMEM((CHUNKS, 3, 2, HALF, LANES), bf),
             pltpu.VMEM((CHUNKS, 2, HALF, LANES), f32),
@@ -493,7 +533,7 @@
             pltpu.VMEM((BR, LANES), f32), pltpu.VMEM((TP, BR, LANES), f32),
             dma((4,)), dma((CHUNKS,)), dma((NX, 2, 2)), dma((NX, 4, 2)), dma((NX, 2)), dma((NX,)),
             dma((NX, 2)), dma((NX, 4)), dma((NX, 3)), dma((CHUNKS,)), dma((CHUNKS,)),
-            dma((CHUNKS, 3)), dma((CHUNKS, 3)), dma((CHUNKS,)), dma((CHUNKS,)),
+            dma((CHUNKS, 3, 2)), dma((CHUNKS, 3, 2)), dma((CHUNKS,)), dma((CHUNKS,)),
             dma((3,)), dma((BR,)), dma((2,)), dma((2,)), dma, dma, dma, dma,
             pltpu.SemaphoreType.REGULAR, pltpu.SemaphoreType.REGULAR,
         ],

time: 84.7 us -> 83.6 us (0.987)
  Pallas kernels: 83.3 us -> 82.2 us
    pallas_call x1, Pallas kernels: 83.3 us -> 82.2 us  [local(): pl.pallas_call(kernel, name='scores', out_shape=jax.ShapeDtypeStruct((BR,...]
where the time goes in v4:
time: 83.6 us; the launch traced here: 83.5 us
  Pallas kernels  82.2 us (98%)
  local copies, waits for them, and re-layouts  1.26 us (2%)
    pallas_call x1, Pallas kernels, local(): pl.pallas_call(kernel, name='scores', out_shape=jax.ShapeDtypeStruct((BR,...  82.2 us

profile of v4, /device:TPU:1, one launch (start us, length us, event | category | flops | bytes accessed | tf_op | source)
XLA Modules:
  0.0 83.5 jit_solution(1834103350758120186)
XLA Ops:
  0.0 82.2 %scores.1 = f32[4,72]{1,0:T(4,128)} custom-call(s32[1,72]{1,0:T(1,128)} %bitcast.5, s32[1,6]{1,0:T(1,128)} %len_ref.1, bf16[72,8192]{1,0:T(8,128)(2,1)} %roll_hbm.1, bf16[1,8192]{1,0:T(2,128)(2,1)} %gain_hbm.1, bf16[1024,512]{1,0:T(8,128)(2,1)} %bitcast.3, bf16[1024,128]{1,0:T(8,128)(2,1)} %bitcast.4, bf16[1,512]{1,0:T(2,128)(2,1)} %hw_hbm.1, ...), custom_call_target="tpu_custom_call" | custom-call | tf_op jit(solution)/shard_map/scores/pallas_call | solution.py:510
  82.2 1.3 %copy.10 = f32[4,72]{1,0:T(4,128)} copy(f32[4,72]{1,0:T(4,128)} %scores.1) | data formatting | bytes 2304

commit v5 on v4

--- a/solution.py
+++ b/solution.py
@@ -27,8 +27,8 @@
 
 
 def kernel(send_ref, len_ref, roll_hbm, gain_hbm, wq_hbm, wkv_hbm, hw_hbm, ha_hbm, out_ref,
-           roll, gain_v, wA, hw_v, ha_v, y, X, N, pf, lsave, pbuf, rbuf, fown, ybuf, qf, kvb, hwf, hwb, bias, tb, rb, zo, zb,
-           ld, lw, xo, xq, so, sd, fo, fq, zn, ws, wr, ps, pr, ys, yr, hs, hr, kvs, kvr, ts, tr, zs, zr, ra, rb4):
+           roll, gain_v, wA, hw_v, ha_v, y, X, N, pf, lsave, pbuf, rbuf, fown, ybuf, qf, kvst, kvb, hwf, hwb, bias, tb, rb, zo, zb,
+           ld, lw, xo, xq, so, sd, fo, fq, zn, ws, wr, ps, pr, ys, yr, hs, hr, kvs, kvr, ts, tr, zs, zr, ra, rb4, rc):
     f32, bf, i32 = jnp.float32, jnp.bfloat16, jnp.int32
     br = lax.axis_index("branch")
     seg = lax.axis_index("segment")
@@ -306,6 +306,43 @@
         ysend(c).start()
         qf[c, yl] = fown[c, yl].astype(bf)
 
+    slot = z // 8
+
+    def kv_rows(part):
+        return pl.ds(64 * part, 64 + 16 * part)
+
+    def kv_here(k, e):
+        return jnp.logical_and(k == yl, 2 * lax.rem(z, 8) + e == z)
+
+    def kv_send(k, e, part):
+        return pltpu.make_async_remote_copy(
+            src_ref=kvst.at[k, kv_rows(part)], dst_ref=kvb.at[slot, yl, kv_rows(part)], send_sem=kvs.at[k, e, part],
+            recv_sem=kvr.at[slot, yl, part], device_id=(br, k * NX + x, 2 * lax.rem(z, 8) + e), device_id_type=MESH)
+
+    def kv_keep(k, part):
+        return pltpu.make_async_copy(
+            kvst.at[k, kv_rows(part)], kvb.at[slot, yl, kv_rows(part)], kvr.at[slot, yl, part])
+
+    def consume_kv(part):
+        rows = kv_rows(part)
+        tot = fown[0, :, rows]
+        for d in range(1, NX):
+            psend(0, d, part).wait_recv()
+            tot = tot + rbuf[0, d - 1, :, rows].astype(f32)
+        kvst[:, rows] = tot.astype(bf)
+        for k in range(2):
+            for e in range(2):
+                @pl.when(kv_here(k, e))
+                def _():
+                    kv_keep(k, part).start()
+
+                @pl.when(jnp.logical_not(kv_here(k, e)))
+                def _():
+                    kv_send(k, e, part).start()
+
+    pl.semaphore_wait(rb4, 2)
+    pl.semaphore_signal(rc, inc=1, device_id=(br, part_seg, z), device_id_type=MESH)
+
     for q in range(2):
         row_wait(0, q, core)
         for d in range(NX):
@@ -331,6 +368,8 @@
             to_sib(xp, q).start()
         if d == 1:
             w_next(4)
+            pl.semaphore_wait(rc, 1)
+            consume_kv(0)
 
     @drains.append
     def _():
@@ -352,29 +391,6 @@
 
     lax.fori_loop(0, NX, norm_far, 0)
 
-    slot = z // 8
-
-    def kv_send(e):
-        return pltpu.make_async_remote_copy(
-            src_ref=qf.at[0], dst_ref=kvb.at[slot], send_sem=kvs.at[e], recv_sem=kvr.at[slot],
-            device_id=(br, seg, 2 * lax.rem(z, 8) + e), device_id_type=MESH)
-
-    keep = pltpu.make_async_copy(qf.at[0], kvb.at[slot], kvr.at[slot])
-
-    def kv_start():
-        pl.semaphore_wait(rb4, 2)
-        ysend(0).wait_recv()
-        for e in range(2):
-            here = 2 * lax.rem(z, 8) + e == z
-
-            @pl.when(here)
-            def _():
-                keep.start()
-
-            @pl.when(jnp.logical_not(here))
-            def _():
-                kv_send(e).start()
-
     def chunk(c, _):
         @pl.when(c >= 2)
         def _():
@@ -383,13 +399,13 @@
 
         produce(c, 1)
 
-        @pl.when(c > 0)
+        @pl.when(c == 1)
+        def _():
+            consume_kv(1)
+
+        @pl.when(c > 1)
         def _():
             consume(c - 1)
-
-        @pl.when(c == 2)
-        def _():
-            kv_start()
         return 0
 
     lax.fori_loop(0, CHUNKS, chunk, 0)
@@ -400,14 +416,19 @@
             for d in range(1, NX):
                 for part in range(2):
                     psend(c, d, part).wait_send()
-            ysend(c).wait_send()
+
+            @pl.when(c > 0)
+            def _():
+                ysend(c).wait_send()
             return 0
 
         lax.fori_loop(0, CHUNKS, drain, 0)
-        for e in range(2):
-            @pl.when(2 * lax.rem(z, 8) + e != z)
-            def _():
-                kv_send(e).wait_send()
+        for k in range(2):
+            for e in range(2):
+                @pl.when(jnp.logical_not(kv_here(k, e)))
+                def _():
+                    for part in range(2):
+                        kv_send(k, e, part).wait_send()
 
     for o in range(1, BR):
         frm = lax.rem(br + o, BR)
@@ -423,7 +444,10 @@
 
     consume(CHUNKS - 1)
     for k in range(2):
-        pltpu.make_async_copy(kvb.at[k], kvb.at[k], kvr.at[k]).wait()
+        for h in range(2):
+            for part in range(2):
+                ref = kvb.at[k, h, kv_rows(part)]
+                pltpu.make_async_copy(ref, ref, kvr.at[k, h, part]).wait()
     keys, values = kvb[0].reshape(PACK, LANES), kvb[1].reshape(PACK, LANES)
     acc = jnp.zeros((PACK, LANES), f32)
     for h in range(HEADS_HERE):
@@ -526,7 +550,7 @@
             pltpu.VMEM((CHUNKS, 2, HALF, LANES), f32),
             pltpu.VMEM((CHUNKS, HALF, LANES), bf),
             pltpu.VMEM((CHUNKS, 2, HALF, LANES), bf),
-            pltpu.VMEM((2, 2, HALF, LANES), bf),
+            pltpu.VMEM((2, HALF, LANES), bf), pltpu.VMEM((2, 2, HALF, LANES), bf),
             pltpu.VMEM((1, WIDTH), f32), pltpu.VMEM((BR, 1, WIDTH), f32),
             pltpu.VMEM((PACK, PACK), f32),
             pltpu.VMEM((32, 1, LANES), f32), pltpu.VMEM((32, 1, LANES), f32),
@@ -534,8 +558,8 @@
             dma((4,)), dma((CHUNKS,)), dma((NX, 2, 2)), dma((NX, 4, 2)), dma((NX, 2)), dma((NX,)),
             dma((NX, 2)), dma((NX, 4)), dma((NX, 3)), dma((CHUNKS,)), dma((CHUNKS,)),
             dma((CHUNKS, 3, 2)), dma((CHUNKS, 3, 2)), dma((CHUNKS,)), dma((CHUNKS,)),
-            dma((3,)), dma((BR,)), dma((2,)), dma((2,)), dma, dma, dma, dma,
-            pltpu.SemaphoreType.REGULAR, pltpu.SemaphoreType.REGULAR,
+            dma((3,)), dma((BR,)), dma((2, 2, 2)), dma((2, 2, 2)), dma, dma, dma, dma,
+            pltpu.SemaphoreType.REGULAR, pltpu.SemaphoreType.REGULAR, pltpu.SemaphoreType.REGULAR,
         ],
         compiler_params=pltpu.CompilerParams(
             collective_id=0, has_side_effects=True, vmem_limit_bytes=56 << 20),

time: 83.6 us -> 84.1 us (level)
  no operation moved by 1% of the time
where the time goes in v5:
time: 84.1 us; the launch traced here: 84 us
  Pallas kernels  82.7 us (98%)
  local copies, waits for them, and re-layouts  1.26 us (1%)
    pallas_call x1, Pallas kernels, local(): pl.pallas_call(kernel, name='scores', out_shape=jax.ShapeDtypeStruct((BR,...  82.7 us

profile of v5, /device:TPU:1, one launch (start us, length us, event | category | flops | bytes accessed | tf_op | source)
XLA Modules:
  0.0 84.0 jit_solution(14384316305970493896)
XLA Ops:
  0.0 82.7 %scores.1 = f32[4,72]{1,0:T(4,128)} custom-call(s32[1,72]{1,0:T(1,128)} %bitcast.5, s32[1,6]{1,0:T(1,128)} %len_ref.1, bf16[72,8192]{1,0:T(8,128)(2,1)} %roll_hbm.1, bf16[1,8192]{1,0:T(2,128)(2,1)} %gain_hbm.1, bf16[1024,512]{1,0:T(8,128)(2,1)} %bitcast.3, bf16[1024,128]{1,0:T(8,128)(2,1)} %bitcast.4, bf16[1,512]{1,0:T(2,128)(2,1)} %hw_hbm.1, ...), custom_call_target="tpu_custom_call" | custom-call | tf_op jit(solution)/shard_map/scores/pallas_call | solution.py:534
  82.7 1.3 %copy.10 = f32[4,72]{1,0:T(4,128)} copy(f32[4,72]{1,0:T(4,128)} %scores.1) | data formatting | bytes 2304

commit v6 on v5

--- a/solution.py
+++ b/solution.py
@@ -131,8 +131,7 @@
         wsend(c - 2).wait_send()
         wsend(c).start()
 
-    for c in range(2):
-        wsend(c).start()
+    wsend(0).start()
 
     def row_send(d, q):
         xd = lax.rem(x + d, NX)
@@ -157,8 +156,7 @@
         pltpu.make_async_copy(ref, ref, xo.at[xs, c, q]).wait()
 
     for d in (1, 3, 2):
-        for q in range(2):
-            row_send(d, q).start()
+        row_send(d, 0).start()
     for q in range(2):
         row_keep(q).start()
         row_side(0, q, y.at[pl.ds(q * SEG + 2 * x, 2)]).start()
@@ -173,8 +171,6 @@
 
     @drains.append
     def _():
-        for d in range(NX):
-            dist(d).wait_send()
         for c in range(CHUNKS - 2, CHUNKS):
             wsend(c).wait_send()
         for d in range(1, NX):
@@ -206,6 +202,12 @@
         start = jnp.where(pq >= end, end, start)
     bias[...] = jnp.where((pk >= start) & (pk <= pq), 0.0, -1e30)
 
+    for d in range(NX):
+        dist(d).wait_send()
+    wsend(1).start()
+    for d in (1, 3, 2):
+        row_send(d, 1).start()
+
     other = 1 - yh
 
     def block(xp, q, c):
@@ -238,8 +240,8 @@
     spread(rb4, 4)
 
     w_next(2)
-    for d in (1, 3, 2):
-        for q in range(2):
+    for q in range(2):
+        for d in (1, 3, 2):
             row_wait(d, q, core)
             row_side(d, q, None).start()
     w_next(3)
@@ -409,6 +411,7 @@
         return 0
 
     lax.fori_loop(0, CHUNKS, chunk, 0)
+    finish()
 
     @drains.append
     def _():

time: 84.1 us -> 84.1 us (level)
  no operation moved by 1% of the time
where the time goes in v6:
time: 84.1 us; the launch traced here: 84 us
  Pallas kernels  82.7 us (98%)
  local copies, waits for them, and re-layouts  1.26 us (1%)
    pallas_call x1, Pallas kernels, local(): pl.pallas_call(kernel, name='scores', out_shape=jax.ShapeDtypeStruct((BR,...  82.7 us

profile of v6, /device:TPU:1, one launch (start us, length us, event | category | flops | bytes accessed | tf_op | source)
XLA Modules:
  0.0 84.0 jit_solution(16375084035418354724)
XLA Ops:
  0.0 82.7 %scores.1 = f32[4,72]{1,0:T(4,128)} custom-call(s32[1,72]{1,0:T(1,128)} %bitcast.5, s32[1,6]{1,0:T(1,128)} %len_ref.1, bf16[72,8192]{1,0:T(8,128)(2,1)} %roll_hbm.1, bf16[1,8192]{1,0:T(2,128)(2,1)} %gain_hbm.1, bf16[1024,512]{1,0:T(8,128)(2,1)} %bitcast.3, bf16[1024,128]{1,0:T(8,128)(2,1)} %bitcast.4, bf16[1,512]{1,0:T(2,128)(2,1)} %hw_hbm.1, ...), custom_call_target="tpu_custom_call" | custom-call | tf_op jit(solution)/shard_map/scores/pallas_call | solution.py:537
  82.7 1.3 %copy.10 = f32[4,72]{1,0:T(4,128)} copy(f32[4,72]{1,0:T(4,128)} %scores.1) | data formatting | bytes 2304

commit v7 on v6

--- a/solution.py
+++ b/solution.py
@@ -372,6 +372,8 @@
             w_next(4)
             pl.semaphore_wait(rc, 1)
             consume_kv(0)
+        if d == 3:
+            lax.fori_loop(2, 3, early, 0)
 
     @drains.append
     def _():
@@ -394,24 +396,23 @@
     lax.fori_loop(0, NX, norm_far, 0)
 
     def chunk(c, _):
-        @pl.when(c >= 2)
+        @pl.when(c >= 3)
         def _():
             wsend(c).wait_recv()
             produce(c, 0)
 
         produce(c, 1)
 
-        @pl.when(c == 1)
+        @pl.when(c == 2)
         def _():
             consume_kv(1)
 
-        @pl.when(c > 1)
+        @pl.when(c > 3)
         def _():
-            consume(c - 1)
+            consume(c - 3)
         return 0
 
     lax.fori_loop(0, CHUNKS, chunk, 0)
-    finish()
 
     @drains.append
     def _():
@@ -445,6 +446,8 @@
         [jnp.concatenate([order_i[s * 8:(s + 1) * 8], order_i[64:72]], axis=0) == lanes16 for s in range(SEG)], axis=1)
     table = table.astype(f32).astype(bf)
 
+    consume(CHUNKS - 3)
+    consume(CHUNKS - 2)
     consume(CHUNKS - 1)
     for k in range(2):
         for h in range(2):

time: 84.1 us -> 80.9 us (0.962)
  Pallas kernels: 82.7 us -> 79.5 us
    pallas_call x1, Pallas kernels: 82.7 us -> 79.5 us  [local(): pl.pallas_call(kernel, name='scores', out_shape=jax.ShapeDtypeStruct((BR,...]
where the time goes in v7:
time: 80.9 us; the launch traced here: 80.8 us
  Pallas kernels  79.5 us (98%)
  local copies, waits for them, and re-layouts  1.26 us (2%)
    pallas_call x1, Pallas kernels, local(): pl.pallas_call(kernel, name='scores', out_shape=jax.ShapeDtypeStruct((BR,...  79.5 us

profile of v7, /device:TPU:1, one launch (start us, length us, event | category | flops | bytes accessed | tf_op | source)
XLA Modules:
  0.0 80.8 jit_solution(11582595556214554084)
XLA Ops:
  0.0 79.5 %scores.1 = f32[4,72]{1,0:T(4,128)} custom-call(s32[1,72]{1,0:T(1,128)} %bitcast.5, s32[1,6]{1,0:T(1,128)} %len_ref.1, bf16[72,8192]{1,0:T(8,128)(2,1)} %roll_hbm.1, bf16[1,8192]{1,0:T(2,128)(2,1)} %gain_hbm.1, bf16[1024,512]{1,0:T(8,128)(2,1)} %bitcast.3, bf16[1024,128]{1,0:T(8,128)(2,1)} %bitcast.4, bf16[1,512]{1,0:T(2,128)(2,1)} %hw_hbm.1, ...), custom_call_target="tpu_custom_call" | custom-call | tf_op jit(solution)/shard_map/scores/pallas_call | solution.py:540
  79.5 1.3 %copy.10 = f32[4,72]{1,0:T(4,128)} copy(f32[4,72]{1,0:T(4,128)} %scores.1) | data formatting | bytes 2304

commit v8 on v7

--- a/solution.py
+++ b/solution.py
@@ -434,6 +434,10 @@
                     for part in range(2):
                         kv_send(k, e, part).wait_send()
 
+    consume(CHUNKS - 3)
+    consume(CHUNKS - 2)
+    consume(CHUNKS - 1)
+
     for o in range(1, BR):
         frm = lax.rem(br + o, BR)
         pltpu.make_async_copy(hwb.at[frm], hwb.at[frm], hr.at[frm]).wait()
@@ -446,9 +450,7 @@
         [jnp.concatenate([order_i[s * 8:(s + 1) * 8], order_i[64:72]], axis=0) == lanes16 for s in range(SEG)], axis=1)
     table = table.astype(f32).astype(bf)
 
-    consume(CHUNKS - 3)
-    consume(CHUNKS - 2)
-    consume(CHUNKS - 1)
+    finish()
     for k in range(2):
         for h in range(2):
             for part in range(2):

time: 80.9 us -> 80.9 us (level)
  no operation moved by 1% of the time
where the time goes in v8:
time: 80.9 us; the launch traced here: 80.8 us
  Pallas kernels  79.5 us (98%)
  local copies, waits for them, and re-layouts  1.26 us (2%)
    pallas_call x1, Pallas kernels, local(): pl.pallas_call(kernel, name='scores', out_shape=jax.ShapeDtypeStruct((BR,...  79.5 us

profile of v8, /device:TPU:1, one launch (start us, length us, event | category | flops | bytes accessed | tf_op | source)
XLA Modules:
  0.0 80.8 jit_solution(6516054432012193113)
XLA Ops:
  0.0 79.5 %scores.1 = f32[4,72]{1,0:T(4,128)} custom-call(s32[1,72]{1,0:T(1,128)} %bitcast.5, s32[1,6]{1,0:T(1,128)} %len_ref.1, bf16[72,8192]{1,0:T(8,128)(2,1)} %roll_hbm.1, bf16[1,8192]{1,0:T(2,128)(2,1)} %gain_hbm.1, bf16[1024,512]{1,0:T(8,128)(2,1)} %bitcast.3, bf16[1024,128]{1,0:T(8,128)(2,1)} %bitcast.4, bf16[1,512]{1,0:T(2,128)(2,1)} %hw_hbm.1, ...), custom_call_target="tpu_custom_call" | custom-call | tf_op jit(solution)/shard_map/scores/pallas_call | solution.py:542
  79.5 1.3 %copy.10 = f32[4,72]{1,0:T(4,128)} copy(f32[4,72]{1,0:T(4,128)} %scores.1) | data formatting | bytes 2304
